TPU v7x, 32 devices: a whole 2x2x4 slice. The times are simulated.
32 devices in a mesh: gx: 4 (over y, x), gy: 2 (over core), gz: 4 (over z).
Axes of the slice: x: 2, y: 2, z: 4, core: 2. Of those that a mesh axis runs over, the one named last changes fastest.
Arguments:
- positions: float32 [3, 16, 8, 8, 128], P(None, 'gx', 'gy', 'gz'), may hold values from 0 to 128, as said below
- grain_radii: float32 [16, 8, 8, 128], P('gx', 'gy', 'gz'), may hold values from 0.4 to 0.6
- film_liquid: float32 [16, 8, 8, 128], P('gx', 'gy', 'gz'), may hold values from 0.5 to 2
- pair_live: int32 [4, 2, 4, 864], P('gx', 'gy', 'gz'), may hold values from 0 to 1, as said below
- partner: int32 [4, 2, 4, 864, 128], P('gx', 'gy', 'gz'), may hold values from 0 to 127, as said below
- rupture: int32 [4, 2, 4, 864, 128], P('gx', 'gy', 'gz'), may hold values from 0 to 1
- volume: float32 [4, 2, 4, 864, 128], P('gx', 'gy', 'gz'), may hold values from 0.005 to 0.05
Outputs:
- forces: float32 [3, 16, 8, 8, 128], P(None, 'gx', 'gy', 'gz')
- film_next: float32 [16, 8, 8, 128], P('gx', 'gy', 'gz')
- volume_next: float32 [4, 2, 4, 864, 128], P('gx', 'gy', 'gz')
Inputs may be any that keep to these rules, and one draw needn't show every extreme that they name: `pair_live`: slot s of a device is 1 only if its tile pair lies inside the grid; every pair of distinct touching tiles is listed at most once over all devices, by one of its two tiles; the slot of a tile with itself (s % 27 = 13) is always 1. partner[s, m] is never m itself. `positions`: the grains of tile (p, q, r) lie in its box, 8 wide along the first dimension and 4 along the others, the boxes side by side from the root; no two grains are closer than 0.5.
All inputs are finite; a program needn't handle non-finite values.
Results may differ from a plain program's by a relative error of at most 0.0003.
Values sent between devices are 32-bit elements; how exact they have to be, the bound alone decides.
A program may use at most 64 MiB of HBM per device.

v0:
```python
import jax
import jax.numpy as jnp
from jax import lax
from jax.sharding import PartitionSpec as P

ABSORB = 0.02
block_tiles = 2


def padded(cells, sides, width):
    for axis, dim in sides:
        count = lax.axis_size(axis)
        ends = count - 1
        head = lax.slice_in_dim(cells, 0, width, axis=dim)
        tail = lax.slice_in_dim(cells, cells.shape[dim] - width, cells.shape[dim], axis=dim)
        cells = jnp.concatenate(
            [
                lax.ppermute(tail, axis, [(i, (i + 1) % count) for i in range(ends)]),
                cells,
                lax.ppermute(head, axis, [((i + 1) % count, i) for i in range(ends)]),
            ],
            axis=dim,
        )
    return cells


def evaluate(pieces):
    anchor, others, centre, active, partner, rupture, volume = pieces
    grains = anchor.shape[-1]
    identity = jnp.eye(grains, dtype=jnp.float32)
    diagonal = identity[None] * centre[:, None, None]
    deltas = [
        anchor[:, component, :, None] - others[:, component, None, :] for component in range(3)
    ]
    squares = deltas[0] * deltas[0] + deltas[1] * deltas[1] + deltas[2] * deltas[2] + diagonal
    distance = jnp.sqrt(squares)
    reach_sum = anchor[:, 3, :, None] + others[:, 3, None, :]
    reduced = anchor[:, 3, :, None] * others[:, 3, None, :] / reach_sum
    intersection = jnp.maximum(reach_sum - distance, 0.0) * (1.0 - diagonal)
    repulse = (
        jnp.sqrt(reduced) * intersection * jnp.sqrt(intersection) / distance * active[:, None, None]
    )
    products = [repulse * member for member in deltas]
    keep_other = (1.0 - centre)[:, None]
    contact_a = jnp.stack([jnp.sum(member, axis=2) for member in products], axis=1)
    contact_b = jnp.stack([-jnp.sum(member, axis=1) * keep_other for member in products], axis=1)
    choose = (partner[:, :, None] == jnp.arange(grains, dtype=jnp.int32)[None, None, :]).astype(
        jnp.float32
    )
    matched = jnp.einsum("ncj,nij->nci", others, choose, precision=lax.Precision.HIGHEST)
    gap_vec = anchor[:, :3] - matched[:, :3]
    spacing = jnp.sqrt(jnp.sum(gap_vec * gap_vec, axis=1))
    radius_sum = anchor[:, 3] + matched[:, 3]
    harmonic = 2.0 * anchor[:, 3] * matched[:, 3] / radius_sum
    scaled_gap = jnp.maximum(spacing - radius_sum, 0.0) * jnp.sqrt(harmonic / volume)
    broken = rupture.astype(jnp.float32)
    intact = active[:, None] * (1.0 - broken)
    tension = (
        intact * harmonic / (1.0 + 1.05 * scaled_gap + 2.5 * scaled_gap * scaled_gap) / spacing
    )
    bridge_force = tension[:, None, :] * gap_vec
    released = active[:, None] * broken * volume
    volume_next = intact * (volume + ABSORB * (anchor[:, 4] + matched[:, 4]))
    liquid_anchor = 0.5 * released - ABSORB * intact * anchor[:, 4]
    liquid_other = 0.5 * released - ABSORB * intact * matched[:, 4]
    reaction = jnp.einsum(
        "nci,nij->ncj",
        jnp.concatenate([bridge_force, liquid_other[:, None]], axis=1),
        choose,
        precision=lax.Precision.HIGHEST,
    )
    anchor_side = jnp.concatenate([contact_a - bridge_force, liquid_anchor[:, None]], axis=1)
    other_side = (
        jnp.concatenate([contact_b, jnp.zeros_like(liquid_anchor)[:, None]], axis=1) + reaction
    )
    return (anchor_side, other_side, volume_next)


def spread_three(terms, axis_dim):
    total = None
    for shift, member in zip((-1, 0, 1), terms):
        widths = [(0, 0)] * member.ndim
        widths[axis_dim] = (1 + shift, 1 - shift)
        widened = jnp.pad(member, widths)
        total = widened if total is None else total + widened
    return total


def fold_rim(values, axis_dim, depth_cells):
    length = values.shape[axis_dim] - 2 * depth_cells - 2
    interior = lax.slice_in_dim(values, depth_cells + 1, depth_cells + 1 + length, axis=axis_dim)
    lower_rim = lax.slice_in_dim(values, depth_cells - 1, depth_cells, axis=axis_dim)
    upper_rim = lax.slice_in_dim(
        values, depth_cells + 2 + length, depth_cells + 3 + length, axis=axis_dim
    )
    head = lax.slice_in_dim(interior, 0, 1, axis=axis_dim) + lower_rim
    middle = lax.slice_in_dim(interior, 1, length - 1, axis=axis_dim)
    tail = lax.slice_in_dim(interior, length - 1, length, axis=axis_dim) + upper_rim
    return jnp.concatenate([head, middle, tail], axis=axis_dim)


def shards(positions, grain_radii, film_liquid, pair_live, partner, rupture, volume):
    extent_x, extent_y, extent_z, grains = grain_radii.shape
    tile_count = extent_x * extent_y * extent_z
    slot_count = 27 * tile_count
    grain_state = jnp.concatenate([positions, grain_radii[None], film_liquid[None]], axis=0)
    border = padded(grain_state, (("gx", 1), ("gy", 2), ("gz", 3)), 1)
    anchor = jnp.repeat(grain_state.reshape(5, tile_count, grains).transpose(1, 0, 2), 27, axis=0)
    facing = []
    for along_x in (-1, 0, 1):
        for along_y in (-1, 0, 1):
            for along_z in (-1, 0, 1):
                start = (0, 1 + along_x, 1 + along_y, 1 + along_z, 0)
                limit = (
                    5,
                    1 + along_x + extent_x,
                    1 + along_y + extent_y,
                    1 + along_z + extent_z,
                    grains,
                )
                facing.append(lax.slice(border, start, limit))
    others = jnp.stack(facing, axis=4).reshape(5, slot_count, grains).transpose(1, 0, 2)
    centre = (jnp.arange(slot_count, dtype=jnp.int32) % 27 == 13).astype(jnp.float32)
    live_flags = pair_live.reshape(slot_count)
    pieces = (
        anchor,
        others,
        centre,
        live_flags.astype(jnp.float32),
        partner.reshape(slot_count, grains),
        rupture.reshape(slot_count, grains),
        volume.reshape(slot_count, grains),
    )
    block_span = 27 * block_tiles
    block_count = slot_count // block_span
    ranking = jnp.argsort(1 - live_flags, stable=True)
    packed = jax.tree.map(lambda member: member[ranking], pieces)
    blocked = jax.tree.map(
        lambda member: member.reshape((block_count, block_span) + member.shape[1:]), packed
    )
    needed = (jnp.sum(live_flags) + block_span - 1) // block_span
    empty = (
        jnp.zeros((block_count, block_span, 4, grains), jnp.float32),
        jnp.zeros((block_count, block_span, 4, grains), jnp.float32),
        jnp.zeros((block_count, block_span, grains), jnp.float32),
    )

    def advance(number, carry):
        piece = jax.tree.map(
            lambda member: lax.dynamic_index_in_dim(member, number, 0, keepdims=False), blocked
        )
        result = evaluate(piece)
        return jax.tree.map(
            lambda held, latest: lax.dynamic_update_index_in_dim(held, latest, number, 0),
            carry,
            result,
        )

    results = lax.fori_loop(0, needed, advance, empty)
    flat = jax.tree.map(lambda member: member.reshape((slot_count,) + member.shape[2:]), results)
    inverse = jnp.argsort(ranking)
    anchor_side, other_side, fresh = jax.tree.map(lambda member: member[inverse], flat)
    own_terms = jnp.sum(anchor_side.reshape(extent_x, extent_y, extent_z, 27, 4, grains), axis=3)
    far_terms = other_side.reshape(extent_x, extent_y, extent_z, 3, 3, 3, 4, grains)
    section_z = spread_three([far_terms[:, :, :, :, :, index] for index in range(3)], 2)
    section_y = spread_three([section_z[:, :, :, :, index] for index in range(3)], 1)
    section_x = spread_three([section_y[:, :, :, index] for index in range(3)], 0)
    gathered = section_x + jnp.pad(own_terms, ((1, 1), (1, 1), (1, 1), (0, 0), (0, 0)))
    totals = gathered.transpose(3, 0, 1, 2, 4)
    widened = padded(totals, (("gx", 1), ("gy", 2), ("gz", 3)), 2)
    folded = fold_rim(fold_rim(fold_rim(widened, 1, 2), 2, 2), 3, 2)
    forces = folded[:3]
    film_next = film_liquid + folded[3]
    volume_next = fresh.reshape(1, 1, 1, slot_count, grains)
    return (forces, film_next, volume_next)


def solution(mesh):
    return jax.shard_map(
        shards,
        mesh=mesh,
        in_specs=(
            P(None, "gx", "gy", "gz", None),
            P("gx", "gy", "gz", None),
            P("gx", "gy", "gz", None),
            P("gx", "gy", "gz", None),
            P("gx", "gy", "gz", None, None),
            P("gx", "gy", "gz", None, None),
            P("gx", "gy", "gz", None, None),
        ),
        out_specs=(
            P(None, "gx", "gy", "gz", None),
            P("gx", "gy", "gz", None),
            P("gx", "gy", "gz", None, None),
        ),
        check_vma=False,
    )
```

profile of v0, /device:TPU:0, one launch (start us, length us, event | category | flops | bytes accessed | tf_op | source)
XLA Modules:
  0.0 282.2 jit_solution(3688791585882860028)
XLA Ops:
  1.6 4.9 %collective-permute-start = (f32[5,1,4,2,128]{4,3,2,1,0:T(2,128)S(1)}, f32[5,1,4,2,128]{4,3,2,1,0:T(2,128)S(1)}, u32[]{:S(2)}, u32[]{:S(2)}) collective-permute-start(f32[5,1,4,2,128]{4,3,2,1,0:T(2,128)S(1)} %get-tuple-element.242), channel_id=1, source_target_pairs={{0,8},{8,16},{16,24},{1,9},{9,17},{17,25},{2,10},{10,18},{18,26},{... | collective-permute-start | bytes 61448 | tf_op jit(solution)/shard_map/ppermute | solution.py:18
  6.5 1.3 collective-permute-start.1
  7.8 1.3 subtract_reduce_fusion
  9.8 4.4 %sort.34 = (s32[864]{0:T(1024)}, s32[864]{0:T(1024)S(1)}) sort(s32[864]{0:T(1024)S(1)} %get-tuple-element.168, s32[864]{0:T(1024)S(1)} %iota.29), dimensions={0}, to_apply=%region_1.2 | sort | flops 8640 | bytes 13824 | tf_op jit(solution)/shard_map/jit(argsort)/sort | solution.py:136
  14.2 4.4 %sort.35 = (s32[864]{0:T(1024)}, s32[864]{0:T(1024)S(1)}) sort(s32[864]{0:T(1024)S(1)} %get-tuple-element.70, s32[864]{0:T(1024)S(1)} %iota.31), dimensions={0}, to_apply=%region_11.12 | sort | flops 8640 | bytes 13824 | tf_op jit(solution)/shard_map/jit(argsort)/sort | solution.py:161
  20.3 1.5 collective-permute-start.2
  21.7 1.3 collective-permute-start.3
  23.8 2.0 broadcast_in_dim.20.clone
  25.8 5.0 %gather_fusion = f32[864,5,128]{2,1,0:T(8,128)} fusion(f32[864,5,128]{2,1,0:T(8,128)} %bitcast.270, s32[1024]{0:T(1024)S(1)} %get-tuple-element.245), kind=kCustom, calls=%fused_computation | custom fusion | bytes 4427136 | tf_op jit(solution)/shard_map/gather | solution.py:137
  30.9 1.9 gather_fusion.4
  32.9 1.9 gather_fusion.6
  35.7 1.9 gather_fusion.5
  38.4 3.7 %gather_fusion.2 = f32[864]{0:T(1024)S(1)} fusion(f32[864]{0:T(1024)S(1)} %fusion.76, s32[1024]{0:T(1024)S(1)} %get-tuple-element.245), kind=kCustom, calls=%fused_computation.2 | custom fusion | bytes 10368 | tf_op jit(solution)/shard_map/gather | solution.py:137
  42.2 3.7 %gather_fusion.3 = f32[864]{0:T(1024)S(1)} fusion(f32[864]{0:T(1024)S(1)} %convert_reduce_fusion, s32[1024]{0:T(1024)S(1)} %get-tuple-element.245), kind=kCustom, calls=%fused_computation.3 | custom fusion | bytes 10368 | tf_op jit(solution)/shard_map/gather | solution.py:137
  46.3 3.5 %collective-permute-start.4 = (f32[5,6,6,1,128]{4,3,2,1,0:T(1,128)S(1)}, f32[5,6,6,1,128]{4,3,2,1,0:T(1,128)S(1)}, u32[]{:S(2)}, u32[]{:S(2)}) collective-permute-start(f32[5,6,6,1,128]{4,3,2,1,0:T(1,128)S(1)} %get-tuple-element.237), channel_id=1, source_target_pairs={{0,1},{1,2},{2,3},{4,5},{5,6},{6,7},{8,9},{9,10},{10,11},{12,13},{... | collective-permute-start | bytes 276488 | tf_op jit(solution)/shard_map/ppermute | solution.py:18
  51.2 1.5 collective-permute-done.4
  52.6 4.4 %collective-permute-done.5 = f32[5,6,6,1,128]{4,3,2,1,0:T(1,128)S(1)} collective-permute-done((f32[5,6,6,1,128]{4,3,2,1,0:T(1,128)S(1)}, f32[5,6,6,1,128]{4,3,2,1,0:T(1,128)S(1)}, u32[]{:S(2)}, u32[]{:S(2)}) %collective-permute-start.5) | collective-permute-done | bytes 92192 | tf_op jit(solution)/shard_map/ppermute | solution.py:20
  58.6 3.2 %copy.86 = f32[5,4,4,2,27,128]{5,0,4,3,2,1:T(8,128)} copy(f32[5,4,4,2,27,128]{5,3,2,1,0,4:T(2,128)S(1)} %fusion.43) | data formatting | bytes 4423680 | tf_op jit(solution)/shard_map/reshape | solution.py:122
  61.8 5.1 %gather_fusion.1 = f32[864,5,128]{2,1,0:T(8,128)} fusion(f32[864,5,128]{2,1,0:T(8,128)} %bitcast.271, s32[1024]{0:T(1024)S(1)} %get-tuple-element.245), kind=kCustom, calls=%fused_computation.1 | custom fusion | bytes 4427136 | tf_op jit(solution)/shard_map/gather | solution.py:137
  67.1 1.5 broadcast.213.clone
  68.6 94.7 %while.14 = (s32[]{:T(128)}, f32[16,54,4,128]{3,2,1,0:T(4,128)S(1)}, f32[16,54,4,128]{3,2,1,0:T(4,128)}, f32[16,54,128]{2,0,1:T(8,128)S(1)}, s32[]{:T(128)}, /*i...) while((s32[]{:T(128)}, ...), condition=%wide.region_10.11_spmd, body=%wide.region_2.10_spmd.sunk | while | flops 124490296 | bytes 4750891 | solution.py:159
  70.7 4.0 %fusion.99 = f32[54,5,128]{2,1,0:T(8,128)S(1)} fusion(f32[54,5,128]{2,1,0:T(8,128)S(1)} %get-tuple-element.348, s32[54,128]{1,0:T(8,128)S(1)} %dynamic-slice_bitcast_fusion.6), kind=kOutput, calls=%fused_computation.33.clone.1 | convolution fusion | flops 53968896 | bytes 304128 | tf_op jit(solution)/shard_map/while/body/ncj,nij->nci/dot_general | solution.py:50
  74.8 1.3 multiply_subtract_fusion.4
  76.5 10.4 %fusion.104 = (f32[54,128]{1,0:T(8,128)S(1)}, f32[54,128]{1,0:T(8,128)S(1)}, f32[54,128]{1,0:T(8,128)S(1)}, f32[54,128]{1,0:T(8,128)S(1)}, f32[54,128]{1,0:T(8,128)S(1)}, /*index=5*/f32[54,128]{1,0:T(8,128)S(1)}) fusion(f32[54,128]{1,0:T(8,128)S(1)} %bitcast.302, f32[54,128]{1,0:T(8,128)S(1)} %bitcast.298, f32[54]{0:T(128)S(1)} %fusion.100, ...), kind=kLoop, calls=%fused_computation.34.clone.1 | loop fusion | flops 26500608 | bytes 453040 | tf_op jit(solution)/shard_map/while/body/reduce_sum | solution.py:46
  87.3 3.8 %fusion.106 = f32[16,54,4,128]{3,2,1,0:T(4,128)} fusion(f32[16,54,4,128]{3,2,1,0:T(4,128)} %get-tuple-element.392, s32[]{:T(128)S(6)} %select_n.55, s32[54,128]{1,0:T(8,128)S(1)} %dynamic-slice_bitcast_fusion.6, f32[54,1,128]{2,1,0:T(1,128)S(1)} %broadcast.331, f32[54,1,128]{2,1,0:T(1,128)S(1)} %get-tuple-element.369, ...), kind=kOutput, calls=%fused_computation.44.clone.1 | convolution fusion | flops 43490304 | bytes 359428 | tf_op jit(solution)/shard_map/while/body/nci,nij->ncj/dot_general | solution.py:66
  94.3 4.0 %fusion.99 = f32[54,5,128]{2,1,0:T(8,128)S(1)} fusion(f32[54,5,128]{2,1,0:T(8,128)S(1)} %get-tuple-element.348, s32[54,128]{1,0:T(8,128)S(1)} %dynamic-slice_bitcast_fusion.6), kind=kOutput, calls=%fused_computation.33.clone.1 | convolution fusion | flops 53968896 | bytes 304128 | tf_op jit(solution)/shard_map/while/body/ncj,nij->nci/dot_general | solution.py:50
  98.4 1.3 multiply_subtract_fusion.4
  100.1 10.4 %fusion.104 = (f32[54,128]{1,0:T(8,128)S(1)}, f32[54,128]{1,0:T(8,128)S(1)}, f32[54,128]{1,0:T(8,128)S(1)}, f32[54,128]{1,0:T(8,128)S(1)}, f32[54,128]{1,0:T(8,128)S(1)}, /*index=5*/f32[54,128]{1,0:T(8,128)S(1)}) fusion(f32[54,128]{1,0:T(8,128)S(1)} %bitcast.302, f32[54,128]{1,0:T(8,128)S(1)} %bitcast.298, f32[54]{0:T(128)S(1)} %fusion.100, ...), kind=kLoop, calls=%fused_computation.34.clone.1 | loop fusion | flops 26500608 | bytes 453040 | tf_op jit(solution)/shard_map/while/body/reduce_sum | solution.py:46
  111.0 3.8 %fusion.106 = f32[16,54,4,128]{3,2,1,0:T(4,128)} fusion(f32[16,54,4,128]{3,2,1,0:T(4,128)} %get-tuple-element.392, s32[]{:T(128)S(6)} %select_n.55, s32[54,128]{1,0:T(8,128)S(1)} %dynamic-slice_bitcast_fusion.6, f32[54,1,128]{2,1,0:T(1,128)S(1)} %broadcast.331, f32[54,1,128]{2,1,0:T(1,128)S(1)} %get-tuple-element.369, ...), kind=kOutput, calls=%fused_computation.44.clone.1 | convolution fusion | flops 43490304 | bytes 359428 | tf_op jit(solution)/shard_map/while/body/nci,nij->ncj/dot_general | solution.py:66
  117.9 4.0 %fusion.99 = f32[54,5,128]{2,1,0:T(8,128)S(1)} fusion(f32[54,5,128]{2,1,0:T(8,128)S(1)} %get-tuple-element.348, s32[54,128]{1,0:T(8,128)S(1)} %dynamic-slice_bitcast_fusion.6), kind=kOutput, calls=%fused_computation.33.clone.1 | convolution fusion | flops 53968896 | bytes 304128 | tf_op jit(solution)/shard_map/while/body/ncj,nij->nci/dot_general | solution.py:50
  122.0 1.3 multiply_subtract_fusion.4
  123.7 10.4 %fusion.104 = (f32[54,128]{1,0:T(8,128)S(1)}, f32[54,128]{1,0:T(8,128)S(1)}, f32[54,128]{1,0:T(8,128)S(1)}, f32[54,128]{1,0:T(8,128)S(1)}, f32[54,128]{1,0:T(8,128)S(1)}, /*index=5*/f32[54,128]{1,0:T(8,128)S(1)}) fusion(f32[54,128]{1,0:T(8,128)S(1)} %bitcast.302, f32[54,128]{1,0:T(8,128)S(1)} %bitcast.298, f32[54]{0:T(128)S(1)} %fusion.100, ...), kind=kLoop, calls=%fused_computation.34.clone.1 | loop fusion | flops 26500608 | bytes 453040 | tf_op jit(solution)/shard_map/while/body/reduce_sum | solution.py:46
  134.6 3.8 %fusion.106 = f32[16,54,4,128]{3,2,1,0:T(4,128)} fusion(f32[16,54,4,128]{3,2,1,0:T(4,128)} %get-tuple-element.392, s32[]{:T(128)S(6)} %select_n.55, s32[54,128]{1,0:T(8,128)S(1)} %dynamic-slice_bitcast_fusion.6, f32[54,1,128]{2,1,0:T(1,128)S(1)} %broadcast.331, f32[54,1,128]{2,1,0:T(1,128)S(1)} %get-tuple-element.369, ...), kind=kOutput, calls=%fused_computation.44.clone.1 | convolution fusion | flops 43490304 | bytes 359428 | tf_op jit(solution)/shard_map/while/body/nci,nij->ncj/dot_general | solution.py:66
  141.5 4.0 %fusion.99 = f32[54,5,128]{2,1,0:T(8,128)S(1)} fusion(f32[54,5,128]{2,1,0:T(8,128)S(1)} %get-tuple-element.348, s32[54,128]{1,0:T(8,128)S(1)} %dynamic-slice_bitcast_fusion.6), kind=kOutput, calls=%fused_computation.33.clone.1 | convolution fusion | flops 53968896 | bytes 304128 | tf_op jit(solution)/shard_map/while/body/ncj,nij->nci/dot_general | solution.py:50
  145.6 1.3 multiply_subtract_fusion.4
  147.3 10.4 %fusion.104 = (f32[54,128]{1,0:T(8,128)S(1)}, f32[54,128]{1,0:T(8,128)S(1)}, f32[54,128]{1,0:T(8,128)S(1)}, f32[54,128]{1,0:T(8,128)S(1)}, f32[54,128]{1,0:T(8,128)S(1)}, /*index=5*/f32[54,128]{1,0:T(8,128)S(1)}) fusion(f32[54,128]{1,0:T(8,128)S(1)} %bitcast.302, f32[54,128]{1,0:T(8,128)S(1)} %bitcast.298, f32[54]{0:T(128)S(1)} %fusion.100, ...), kind=kLoop, calls=%fused_computation.34.clone.1 | loop fusion | flops 26500608 | bytes 453040 | tf_op jit(solution)/shard_map/while/body/reduce_sum | solution.py:46
  158.2 3.8 %fusion.106 = f32[16,54,4,128]{3,2,1,0:T(4,128)} fusion(f32[16,54,4,128]{3,2,1,0:T(4,128)} %get-tuple-element.392, s32[]{:T(128)S(6)} %select_n.55, s32[54,128]{1,0:T(8,128)S(1)} %dynamic-slice_bitcast_fusion.6, f32[54,1,128]{2,1,0:T(1,128)S(1)} %broadcast.331, f32[54,1,128]{2,1,0:T(1,128)S(1)} %get-tuple-element.369, ...), kind=kOutput, calls=%fused_computation.44.clone.1 | convolution fusion | flops 43490304 | bytes 359428 | tf_op jit(solution)/shard_map/while/body/nci,nij->ncj/dot_general | solution.py:66
  164.5 3.7 %gather_fusion.7 = f32[864,4,128]{2,1,0:T(4,128)S(1)} fusion(f32[864,4,128]{2,1,0:T(4,128)} %bitcast.274, s32[1024]{0:T(1024)S(1)} %get-tuple-element.244), kind=kCustom, calls=%fused_computation.7 | custom fusion | bytes 3542400 | tf_op jit(solution)/shard_map/gather | solution.py:162
  170.4 4.0 %gather_fusion.8 = f32[864,4,128]{2,1,0:T(4,128)} fusion(f32[864,4,128]{2,1,0:T(4,128)S(1)} %bitcast.273, s32[1024]{0:T(1024)S(1)} %get-tuple-element.244), kind=kCustom, calls=%fused_computation.8 | custom fusion | bytes 3542400 | tf_op jit(solution)/shard_map/gather | solution.py:162
  174.3 1.7 reduce_sum.82
  176.2 4.4 %collective-permute-start.6 = (f32[4,2,6,4,128]{4,0,3,2,1:T(4,128)S(1)}, f32[4,2,6,4,128]{4,0,3,2,1:T(4,128)S(1)}, u32[]{:S(2)}, u32[]{:S(2)}) collective-permute-start(f32[4,2,6,4,128]{4,0,3,2,1:T(4,128)S(1)} %get-tuple-element.230), channel_id=1, source_target_pairs={{0,8},{8,16},{16,24},{1,9},{9,17},{17,25},{2,10},{10,18},{18,26},{... | collective-permute-start | bytes 294920 | tf_op jit(solution)/shard_map/ppermute | solution.py:18
  182.7 4.3 %collective-permute-done.7 = f32[4,2,6,4,128]{4,0,3,2,1:T(4,128)S(1)} collective-permute-done((f32[4,2,6,4,128]{4,0,3,2,1:T(4,128)S(1)}, f32[4,2,6,4,128]{4,0,3,2,1:T(4,128)S(1)}, u32[]{:S(2)}, u32[]{:S(2)}) %collective-permute-start.7) | collective-permute-done | bytes 98336 | tf_op jit(solution)/shard_map/ppermute | solution.py:20
  187.2 21.3 %collective-permute-start.8 = (f32[4,10,2,4,128]{4,0,3,2,1:T(4,128)S(1)}, f32[4,10,2,4,128]{4,0,3,2,1:T(4,128)S(1)}, u32[]{:S(2)}, u32[]{:S(2)}) collective-permute-start(f32[4,10,2,4,128]{4,0,3,2,1:T(4,128)S(1)} %get-tuple-element.228), channel_id=1, source_target_pairs={{0,4},{1,5},{2,6},{3,7},{8,12},{9,13},{10,14},{11,15},{16,20},{17,... | collective-permute-start | bytes 491528 | tf_op jit(solution)/shard_map/ppermute | solution.py:18
  209.7 2.0 collective-permute-done.9
  213.0 54.2 %collective-permute-start.10 = (f32[4,10,10,2,128]{4,0,3,2,1:T(4,128)}, f32[4,10,10,2,128]{4,0,3,2,1:T(4,128)S(1)}, u32[]{:S(2)}, u32[]{:S(2)}) collective-permute-start(f32[4,10,10,2,128]{4,0,3,2,1:T(4,128)} %get-tuple-element.221), channel_id=1, source_target_pairs={{0,1},{1,2},{2,3},{4,5},{5,6},{6,7},{8,9},{9,10},{10,11},{12,13},{... | collective-permute-start | bytes 1228808 | tf_op jit(solution)/shard_map/ppermute | solution.py:18
  268.6 2.8 gather_fusion.9
  271.4 5.0 %collective-permute-done.10 = f32[4,10,10,2,128]{4,0,3,2,1:T(4,128)S(1)} collective-permute-done((f32[4,10,10,2,128]{4,0,3,2,1:T(4,128)}, f32[4,10,10,2,128]{4,0,3,2,1:T(4,128)S(1)}, u32[]{:S(2)}, u32[]{:S(2)}) %collective-permute-start.10) | collective-permute-done | bytes 409632 | tf_op jit(solution)/shard_map/ppermute | solution.py:18
  276.4 4.0 %collective-permute-done.11 = f32[4,10,10,2,128]{4,0,3,2,1:T(4,128)S(1)} collective-permute-done((f32[4,10,10,2,128]{4,0,3,2,1:T(4,128)}, f32[4,10,10,2,128]{4,0,3,2,1:T(4,128)S(1)}, u32[]{:S(2)}, u32[]{:S(2)}) %collective-permute-start.11) | collective-permute-done | bytes 409632 | tf_op jit(solution)/shard_map/ppermute | solution.py:20
  (220 shorter events, 35.6 us)
Async XLA Ops:
  0.6 30.2 %copy-start = (s32[1,1,1,864,128]{4,3,2,1,0:T(8,128)S(1)}, s32[1,1,1,864,128]{4,3,2,1,0:T(8,128)}, u32[]{:S(2)}) copy-start(s32[1,1,1,864,128]{4,3,2,1,0:T(8,128)} %param.14) | copy-start | bytes 1327108
  1.6 17.8 %collective-permute-start = (f32[5,1,4,2,128]{4,3,2,1,0:T(2,128)S(1)}, f32[5,1,4,2,128]{4,3,2,1,0:T(2,128)S(1)}, u32[]{:S(2)}, u32[]{:S(2)}) collective-permute-start(f32[5,1,4,2,128]{4,3,2,1,0:T(2,128)S(1)} %get-tuple-element.242), channel_id=1, source_target_pairs={{0,8},{8,16},{16,24},{1,9},{9,17},{17,25},{2,10},{10,18},{18,26},{... | collective-permute-start | bytes 61448 | tf_op jit(solution)/shard_map/ppermute | solution.py:18
  6.5 13.0 %collective-permute-start.1 = (f32[5,1,4,2,128]{4,3,2,1,0:T(2,128)S(1)}, f32[5,1,4,2,128]{4,3,2,1,0:T(2,128)S(1)}, u32[]{:S(2)}, u32[]{:S(2)}) collective-permute-start(f32[5,1,4,2,128]{4,3,2,1,0:T(2,128)S(1)} %get-tuple-element.243), channel_id=1, source_target_pairs={{8,0},{16,8},{24,16},{9,1},{17,9},{25,17},{10,2},{18,10},{26,18},{... | collective-permute-start | bytes 61448 | tf_op jit(solution)/shard_map/ppermute | solution.py:20
  20.3 25.7 %collective-permute-start.2 = (f32[5,6,1,2,128]{4,3,2,1,0:T(2,128)S(1)}, f32[5,6,1,2,128]{4,3,2,1,0:T(2,128)S(1)}, u32[]{:S(2)}, u32[]{:S(2)}) collective-permute-start(f32[5,6,1,2,128]{4,3,2,1,0:T(2,128)S(1)} %get-tuple-element.240), channel_id=1, source_target_pairs={{0,4},{1,5},{2,6},{3,7},{8,12},{9,13},{10,14},{11,15},{16,20},{17,... | collective-permute-start | bytes 92168 | tf_op jit(solution)/shard_map/ppermute | solution.py:18
  21.7 24.2 %collective-permute-start.3 = (f32[5,6,1,2,128]{4,3,2,1,0:T(2,128)S(1)}, f32[5,6,1,2,128]{4,3,2,1,0:T(2,128)S(1)}, u32[]{:S(2)}, u32[]{:S(2)}) collective-permute-start(f32[5,6,1,2,128]{4,3,2,1,0:T(2,128)S(1)} %get-tuple-element.241), channel_id=1, source_target_pairs={{4,0},{5,1},{6,2},{7,3},{12,8},{13,9},{14,10},{15,11},{20,16},{21,... | collective-permute-start | bytes 92168 | tf_op jit(solution)/shard_map/ppermute | solution.py:20
  30.9 2.0 copy-start.1
  32.9 2.8 copy-start.2
  42.1 3.9 %copy-start.5 = (f32[3,4,4,2,128]{4,3,2,1,0:T(2,128)S(1)}, f32[3,4,4,2,128]{4,3,2,1,0:T(2,128)}, u32[]{:S(2)}) copy-start(f32[3,4,4,2,128]{4,3,2,1,0:T(2,128)} %param.9) | copy-start | bytes 147460
  42.1 3.9 %copy-start.6 = (f32[4,4,2,128]{3,2,1,0:T(2,128)S(1)}, f32[4,4,2,128]{3,2,1,0:T(2,128)}, u32[]{:S(2)}) copy-start(f32[4,4,2,128]{3,2,1,0:T(2,128)} %param.11) | copy-start | bytes 49156
  42.1 3.9 %copy-start.7 = (f32[4,4,2,128]{3,2,1,0:T(2,128)S(1)}, f32[4,4,2,128]{3,2,1,0:T(2,128)}, u32[]{:S(2)}) copy-start(f32[4,4,2,128]{3,2,1,0:T(2,128)} %param.10) | copy-start | bytes 49156
  46.3 6.4 %collective-permute-start.4 = (f32[5,6,6,1,128]{4,3,2,1,0:T(1,128)S(1)}, f32[5,6,6,1,128]{4,3,2,1,0:T(1,128)S(1)}, u32[]{:S(2)}, u32[]{:S(2)}) collective-permute-start(f32[5,6,6,1,128]{4,3,2,1,0:T(1,128)S(1)} %get-tuple-element.237), channel_id=1, source_target_pairs={{0,1},{1,2},{2,3},{4,5},{5,6},{6,7},{8,9},{9,10},{10,11},{12,13},{... | collective-permute-start | bytes 276488 | tf_op jit(solution)/shard_map/ppermute | solution.py:18
  49.8 7.3 %collective-permute-start.5 = (f32[5,6,6,1,128]{4,3,2,1,0:T(1,128)S(1)}, f32[5,6,6,1,128]{4,3,2,1,0:T(1,128)S(1)}, u32[]{:S(2)}, u32[]{:S(2)}) collective-permute-start(f32[5,6,6,1,128]{4,3,2,1,0:T(1,128)S(1)} %get-tuple-element.236), channel_id=1, source_target_pairs={{1,0},{2,1},{3,2},{5,4},{6,5},{7,6},{9,8},{10,9},{11,10},{13,12},{... | collective-permute-start | bytes 276488 | tf_op jit(solution)/shard_map/ppermute | solution.py:20
  163.3 1.2 copy-start.3
  168.9 1.5 copy-start.4
  176.2 6.6 %collective-permute-start.6 = (f32[4,2,6,4,128]{4,0,3,2,1:T(4,128)S(1)}, f32[4,2,6,4,128]{4,0,3,2,1:T(4,128)S(1)}, u32[]{:S(2)}, u32[]{:S(2)}) collective-permute-start(f32[4,2,6,4,128]{4,0,3,2,1:T(4,128)S(1)} %get-tuple-element.230), channel_id=1, source_target_pairs={{0,8},{8,16},{16,24},{1,9},{9,17},{17,25},{2,10},{10,18},{18,26},{... | collective-permute-start | bytes 294920 | tf_op jit(solution)/shard_map/ppermute | solution.py:18
  180.6 6.5 %collective-permute-start.7 = (f32[4,2,6,4,128]{4,0,3,2,1:T(4,128)S(1)}, f32[4,2,6,4,128]{4,0,3,2,1:T(4,128)S(1)}, u32[]{:S(2)}, u32[]{:S(2)}) collective-permute-start(f32[4,2,6,4,128]{4,0,3,2,1:T(4,128)S(1)} %get-tuple-element.231), channel_id=1, source_target_pairs={{8,0},{16,8},{24,16},{9,1},{17,9},{25,17},{10,2},{18,10},{26,18},{... | collective-permute-start | bytes 294920 | tf_op jit(solution)/shard_map/ppermute | solution.py:20
  187.2 22.6 %collective-permute-start.8 = (f32[4,10,2,4,128]{4,0,3,2,1:T(4,128)S(1)}, f32[4,10,2,4,128]{4,0,3,2,1:T(4,128)S(1)}, u32[]{:S(2)}, u32[]{:S(2)}) collective-permute-start(f32[4,10,2,4,128]{4,0,3,2,1:T(4,128)S(1)} %get-tuple-element.228), channel_id=1, source_target_pairs={{0,4},{1,5},{2,6},{3,7},{8,12},{9,13},{10,14},{11,15},{16,20},{17,... | collective-permute-start | bytes 491528 | tf_op jit(solution)/shard_map/ppermute | solution.py:18
  208.4 3.3 %collective-permute-start.9 = (f32[4,10,2,4,128]{4,0,3,2,1:T(4,128)S(1)}, f32[4,10,2,4,128]{4,0,3,2,1:T(4,128)S(1)}, u32[]{:S(2)}, u32[]{:S(2)}) collective-permute-start(f32[4,10,2,4,128]{4,0,3,2,1:T(4,128)S(1)} %get-tuple-element.229), channel_id=1, source_target_pairs={{4,0},{5,1},{6,2},{7,3},{12,8},{13,9},{14,10},{15,11},{20,16},{21,... | collective-permute-start | bytes 491528 | tf_op jit(solution)/shard_map/ppermute | solution.py:20
  213.0 63.5 %collective-permute-start.10 = (f32[4,10,10,2,128]{4,0,3,2,1:T(4,128)}, f32[4,10,10,2,128]{4,0,3,2,1:T(4,128)S(1)}, u32[]{:S(2)}, u32[]{:S(2)}) collective-permute-start(f32[4,10,10,2,128]{4,0,3,2,1:T(4,128)} %get-tuple-element.221), channel_id=1, source_target_pairs={{0,1},{1,2},{2,3},{4,5},{5,6},{6,7},{8,9},{9,10},{10,11},{12,13},{... | collective-permute-start | bytes 1228808 | tf_op jit(solution)/shard_map/ppermute | solution.py:18
  267.1 13.3 %collective-permute-start.11 = (f32[4,10,10,2,128]{4,0,3,2,1:T(4,128)}, f32[4,10,10,2,128]{4,0,3,2,1:T(4,128)S(1)}, u32[]{:S(2)}, u32[]{:S(2)}) collective-permute-start(f32[4,10,10,2,128]{4,0,3,2,1:T(4,128)} %get-tuple-element.222), channel_id=1, source_target_pairs={{1,0},{2,1},{3,2},{5,4},{6,5},{7,6},{9,8},{10,9},{11,10},{13,12},{... | collective-permute-start | bytes 1228808 | tf_op jit(solution)/shard_map/ppermute | solution.py:20
where the time goes:
time: 284 us; the launch traced here: 282 us
  starting transfers between devices  97.4 us (34%)
  other arithmetic  71.2 us (25%)
  local copies, waits for them, and re-layouts  57.2 us (20%)
  matrix products  31.1 us (11%)
  waiting for transfers between devices  22.1 us (8%)
    ppermute x6, starting transfers between devices, padded(): lax.ppermute(tail, axis, [(i, (i + 1) % count) for i in range(ends)])  89.6 us
    reduce_sum x4, other arithmetic, evaluate(): jnp.sum(member, axis=1)  41.7 us
    gather x7, local copies, waits for them, and re-layouts, shards(): packed = jax.tree.map(lambda member: member[ranking], pieces)  23.1 us
    dot_general x4, matrix products, evaluate(): jnp.einsum('ncj,nij->nci', others, choose, precision=lax.Precision.HIGHEST)  15.8 us
    dot_general x4, matrix products, evaluate(): jnp.einsum('nci,nij->ncj', jnp.concatenate([bridge_force, liquid_other[:,...  15.3 us
    ppermute x6, waiting for transfers between devices, padded(): lax.ppermute(head, axis, [((i + 1) % count, i) for i in range(ends)])  14.8 us
    gather x3, local copies, waits for them, and re-layouts, shards(): member[inverse]  10.4 us
    ppermute x6, starting transfers between devices, padded(): lax.ppermute(head, axis, [((i + 1) % count, i) for i in range(ends)])  7.75 us
  transfers between devices with their start and end apart: 12, of which 7 were waited for; matrix products, arithmetic and copies ran while one was open for 13% of the time, Pallas kernels for 0%

commit v1 on v0

v1 whole, which is shorter than its diff:
```python
import functools

import jax
import jax.numpy as jnp
from jax import lax
from jax.experimental import pallas as pl
from jax.experimental.pallas import tpu as pltpu
from jax.sharding import PartitionSpec as P

ABSORB = 0.02
TINY = 1e-30
FLOOR = 1e-12


def padded(cells, sides, width):
    for axis, dim in sides:
        count = lax.axis_size(axis)
        ends = count - 1
        head = lax.slice_in_dim(cells, 0, width, axis=dim)
        tail = lax.slice_in_dim(cells, cells.shape[dim] - width, cells.shape[dim], axis=dim)
        cells = jnp.concatenate(
            [
                lax.ppermute(tail, axis, [(i, (i + 1) % count) for i in range(ends)]),
                cells,
                lax.ppermute(head, axis, [((i + 1) % count, i) for i in range(ends)]),
            ],
            axis=dim,
        )
    return cells


def fold(totals, sides):
    for axis, dim in sides:
        count = lax.axis_size(axis)
        ends = count - 1
        size = totals.shape[dim]
        low = lax.slice_in_dim(totals, 0, 1, axis=dim)
        high = lax.slice_in_dim(totals, size - 1, size, axis=dim)
        inner = lax.slice_in_dim(totals, 1, size - 1, axis=dim)
        from_left = lax.ppermute(high, axis, [(i, (i + 1) % count) for i in range(ends)])
        from_right = lax.ppermute(low, axis, [((i + 1) % count, i) for i in range(ends)])
        length = size - 2
        widths = [(0, 0)] * totals.ndim
        widths[dim] = (0, length - 1)
        other = [(0, 0)] * totals.ndim
        other[dim] = (length - 1, 0)
        totals = inner + jnp.pad(from_left, widths) + jnp.pad(from_right, other)
    return totals


def split(values):
    high = values.astype(jnp.bfloat16)
    low = (values - high.astype(jnp.float32)).astype(jnp.bfloat16)
    return high, low


def kernel(
    dims,
    live_smem,
    border_ref,
    flags_ref,
    partner_ref,
    rupture_ref,
    volume_ref,
    totals_ref,
    fresh_ref,
    rows,
    table,
    others,
    held,
    acc,
    far,
    near,
    listed,
):
    bx, by, bz, grains = dims
    wy, wz = by + 2, bz + 2
    blocks = grains // 8
    plane = by * bz
    step = pl.program_id(0)
    cells = (bx + 2) * wy * wz

    @pl.when(step == 0)
    def _():
        far[...] = jnp.zeros_like(far)
        near[...] = jnp.zeros_like(near)
        held[...] = jnp.zeros_like(held)
        others[...] = jnp.full_like(others, 1.0)
        for ix in range(bx + 2):
            for iy in range(wy):
                base = (ix * wy + iy) * wz
                for c in range(5):
                    rows[c, base : base + wz, :] = border_ref[c, ix, iy]
                rows[5, base : base + wz, :] = 1.0 / jnp.maximum(border_ref[3, ix, iy], 0.1)

    def tile_step(local, carry):
        iy = local // bz
        iz = local % bz
        cell = ((step + 1) * wy + iy + 1) * wz + iz + 1
        first = local * 27
        count = jnp.int32(0)
        for s in range(27):
            listed[count] = s
            count = count + live_smem[(step * plane + local) * 27 + s]
        own = [rows[c, pl.ds(cell, 1), :] for c in range(6)]
        pad_rows = jnp.zeros((2, grains), jnp.float32)
        columns = jnp.concatenate([own[0], own[1], own[2], own[3], own[5], own[4], pad_rows], 0).T
        for c in range(5):
            table[c] = jnp.broadcast_to(columns[:, c : c + 1], (grains, grains))
        for ex in range(3):
            for ey in range(3):
                start = cell + ((ex - 1) * wy + (ey - 1)) * wz - 1
                at = ex * 9 + ey * 3
                for c in range(5):
                    others[c, at : at + 3, :] = rows[c, pl.ds(start, 3), :]
        partner = partner_ref[pl.ds(first, 27), :]
        got = [jnp.take_along_axis(others[c, 0:27, :], partner, axis=1) for c in range(5)]
        gap = [own[c] - got[c] for c in range(3)]
        spacing = jnp.sqrt(gap[0] * gap[0] + gap[1] * gap[1] + gap[2] * gap[2])
        radius_sum = own[3] + got[3]
        harmonic = 2.0 * own[3] * got[3] / radius_sum
        vol = volume_ref[pl.ds(first, 27), :]
        scaled = jnp.maximum(spacing - radius_sum, 0.0) * jnp.sqrt(harmonic / vol)
        active = flags_ref[pl.ds(first, 27), :]
        broken = rupture_ref[pl.ds(first, 27), :].astype(jnp.float32)
        intact = active * (1.0 - broken)
        tension = jnp.where(
            intact > 0.0, harmonic / (1.0 + 1.05 * scaled + 2.5 * scaled * scaled) / spacing, 0.0
        )
        force = [tension * member for member in gap]
        released = 0.5 * active * broken * vol
        fresh_ref[pl.ds(first, 27), :] = intact * (vol + ABSORB * (own[4] + got[4]))
        liquid_a = released - ABSORB * intact * own[4]
        liquid_b = released - ABSORB * intact * got[4]
        for c, member in enumerate(force + [liquid_b]):
            held[pl.ds(c, 27, stride=8), :] = member
        anchor_sums = [-jnp.sum(member, axis=0, keepdims=True) for member in force]
        anchor_sums.append(jnp.sum(liquid_a, axis=0, keepdims=True))
        acc[...] = jnp.zeros_like(acc)
        lanes = lax.broadcasted_iota(jnp.int32, (grains, grains), 0)

        def slot_step(k, carry):
            s = listed[k]
            target = cell + (s // 9 - 1) * (wy * wz) + (s // 3 % 3 - 1) * wz + (s % 3 - 1)
            values = held[pl.ds(pl.multiple_of(s * 8, 8), 8), :]
            high, low = split(values)
            chosen = (lanes == partner_ref[pl.ds(first + s, 1), :]).astype(jnp.float32)
            moved = lax.dot_general(
                jnp.concatenate([high, low], 0),
                chosen.astype(jnp.bfloat16),
                (((1,), (1,)), ((), ())),
                preferred_element_type=jnp.float32,
            )
            near[target] += moved[0:8] + moved[8:16]
            x, y, z, r, q = [
                jnp.broadcast_to(rows[c, pl.ds(target, 1), :], (8, grains)) for c in (0, 1, 2, 3, 5)
            ]
            sums = [jnp.zeros((8, grains), jnp.float32)] * 3
            for m in range(blocks):
                part = slice(8 * m, 8 * m + 8)
                dx = table[0, part] - x
                dy = table[1, part] - y
                dz = table[2, part] - z
                square = jnp.maximum(dx * dx + dy * dy + dz * dz, FLOOR)
                inverse = lax.rsqrt(square)
                inter = jnp.maximum(table[3, part] + r - square * inverse, TINY)
                push = inter * inter * inverse * lax.rsqrt(inter * (table[4, part] + q))
                for c, member in enumerate((dx, dy, dz)):
                    product = push * member
                    acc[c, part] += product
                    sums[c] = sums[c] + product
            keep = jnp.where(s == 13, 0.0, 1.0)
            for c in range(3):
                far[target, c] += sums[c] * keep
            return carry

        lax.fori_loop(0, count, slot_step, 0)
        ones = jnp.ones((8, grains), jnp.bfloat16)
        row = lax.broadcasted_iota(jnp.int32, (8, grains), 0)
        added = jnp.zeros((8, grains), jnp.float32)
        for c in range(4):
            value = anchor_sums[c]
            if c < 3:
                high, low = split(acc[c])
                dims_t = (((1,), (1,)), ((), ()))
                value = value + lax.dot_general(
                    ones, high, dims_t, preferred_element_type=jnp.float32
                )
                value = value + lax.dot_general(
                    ones, low, dims_t, preferred_element_type=jnp.float32
                )
            added = added + jnp.where(row == c, value, 0.0)
        near[cell] += added
        return carry

    lax.fori_loop(0, plane, tile_step, 0)

    @pl.when(step == pl.num_programs(0) - 1)
    def _():
        row = lax.broadcasted_iota(jnp.int32, (8, grains), 0)

        def finish(cell, carry):
            value = near[cell]
            for c in range(3):
                total = jnp.sum(far[cell, c], axis=0, keepdims=True)
                value = value - jnp.where(row == c, total, 0.0)
            totals_ref[cell] = value
            return carry

        lax.fori_loop(0, cells, finish, 0)


def shards(positions, grain_radii, film_liquid, pair_live, partner, rupture, volume):
    bx, by, bz, grains = grain_radii.shape
    tiles = bx * by * bz
    slots = 27 * tiles
    cells = (bx + 2) * (by + 2) * (bz + 2)
    state = jnp.concatenate([positions, grain_radii[None], film_liquid[None]], axis=0)
    sides = (("gx", 1), ("gy", 2), ("gz", 3))
    border = padded(state, sides, 1)
    live = pair_live.reshape(slots)
    flags = jnp.broadcast_to(live.astype(jnp.float32)[:, None], (slots, grains))
    span = 27 * by * bz
    wide = pl.BlockSpec((span, grains), lambda i, _: (i, 0))
    height = -(-cells // 8) * 8
    totals, fresh = pl.pallas_call(
        functools.partial(kernel, (bx, by, bz, grains)),
        grid_spec=pltpu.PrefetchScalarGridSpec(
            num_scalar_prefetch=1,
            grid=(bx,),
            in_specs=[
                pl.BlockSpec(border.shape, lambda i, _: (0, 0, 0, 0, 0)),
                wide,
                wide,
                wide,
                wide,
            ],
            out_specs=[pl.BlockSpec((cells, 8, grains), lambda i, _: (0, 0, 0)), wide],
            scratch_shapes=[
                pltpu.VMEM((6, height, grains), jnp.float32),
                pltpu.VMEM((5, grains, grains), jnp.float32),
                pltpu.VMEM((5, 32, grains), jnp.float32),
                pltpu.VMEM((8 * 32, grains), jnp.float32),
                pltpu.VMEM((3, grains, grains), jnp.float32),
                pltpu.VMEM((cells, 3, 8, grains), jnp.float32),
                pltpu.VMEM((cells, 8, grains), jnp.float32),
                pltpu.SMEM((32,), jnp.int32),
            ],
        ),
        out_shape=[
            jax.ShapeDtypeStruct((cells, 8, grains), jnp.float32),
            jax.ShapeDtypeStruct((slots, grains), jnp.float32),
        ],
        name="slots",
    )(
        live,
        border,
        flags,
        partner.reshape(slots, grains),
        rupture.reshape(slots, grains),
        volume.reshape(slots, grains),
    )
    totals = totals.reshape(bx + 2, by + 2, bz + 2, 8, grains)[:, :, :, :4]
    folded = fold(totals, (("gz", 2), ("gy", 1), ("gx", 0))).transpose(3, 0, 1, 2, 4)
    return (folded[:3], film_liquid + folded[3], fresh.reshape(1, 1, 1, slots, grains))


def solution(mesh):
    return jax.shard_map(
        shards,
        mesh=mesh,
        in_specs=(
            P(None, "gx", "gy", "gz", None),
            P("gx", "gy", "gz", None),
            P("gx", "gy", "gz", None),
            P("gx", "gy", "gz", None),
            P("gx", "gy", "gz", None, None),
            P("gx", "gy", "gz", None, None),
            P("gx", "gy", "gz", None, None),
        ),
        out_specs=(
            P(None, "gx", "gy", "gz", None),
            P("gx", "gy", "gz", None),
            P("gx", "gy", "gz", None, None),
        ),
        check_vma=False,
    )
```

time: 284 us -> 137 us (0.48)
  other arithmetic: 71.2 us -> 2.8 us
  local copies, waits for them, and re-layouts: 57.2 us -> 4.48 us
  Pallas kernels: 0 us -> 50.8 us
  starting transfers between devices: 97.4 us -> 55 us
  matrix products: 31.1 us -> 0 us
    ppermute x6 -> x3, starting transfers between devices: 89.6 us -> 9.65 us  [padded(): lax.ppermute(tail, axis, [(i, (i + 1) % count) for i in range(ends)])]
    pallas_call x0 -> x1, Pallas kernels: none -> 50.8 us  [shards(): pl.pallas_call(functools.partial(kernel, (bx, by, bz, grains)), grid_spec...]
    reduce_sum x9 -> x0, other arithmetic: 43.8 us -> none  [the longest x4 41.7 us: evaluate(): jnp.sum(member, axis=1)]
    ppermute x0 -> x6, starting transfers between devices: none -> 41.5 us  [the longest x3 37.6 us: fold(): lax.ppermute(high, axis, [(i, (i + 1) % count) for i in range(ends)])]
    gather x10 -> x0, local copies, waits for them, and re-layouts: 33.5 us -> none  [the longest x7 23.1 us: shards(): packed = jax.tree.map(lambda member: member[ranking], pieces)]
    dot_general x8 -> x0, matrix products: 31.1 us -> none  [the longest x4 15.8 us: evaluate(): jnp.einsum('ncj,nij->nci', others, choose, precision=lax.Precision.HIGHEST)]
    ppermute x0 -> x6, waiting for transfers between devices: none -> 10.3 us  [the longest x3 9.25 us: fold(): lax.ppermute(low, axis, [((i + 1) % count, i) for i in range(ends)])]
    sort x2 -> x0, other arithmetic: 8.75 us -> none  [the longest x1 4.38 us: shards(): inverse = jnp.argsort(ranking)]
  transfers between devices with their start and end apart: 12 -> 12, of which waited for: 7 -> 9; matrix products, arithmetic and copies ran while one was open for 13% -> 1% of each run, Pallas kernels for 0% -> 0%
where the time goes in v1:
time: 137 us; the launch traced here: 135 us
  starting transfers between devices  55 us (40%)
  Pallas kernels  50.8 us (37%)
  waiting for transfers between devices  21 us (15%)
  local copies, waits for them, and re-layouts  4.48 us (3%)
  other arithmetic  2.8 us (2%)
    pallas_call x1, Pallas kernels, shards(): pl.pallas_call(functools.partial(kernel, (bx, by, bz, grains)), grid_spec...  50.8 us
    ppermute x3, starting transfers between devices, fold(): lax.ppermute(high, axis, [(i, (i + 1) % count) for i in range(ends)])  37.6 us
    ppermute x3, waiting for transfers between devices, padded(): lax.ppermute(head, axis, [((i + 1) % count, i) for i in range(ends)])  10.2 us
    ppermute x3, starting transfers between devices, padded(): lax.ppermute(tail, axis, [(i, (i + 1) % count) for i in range(ends)])  9.65 us
    ppermute x3, waiting for transfers between devices, fold(): lax.ppermute(low, axis, [((i + 1) % count, i) for i in range(ends)])  9.25 us
    ppermute x3, starting transfers between devices, padded(): lax.ppermute(head, axis, [((i + 1) % count, i) for i in range(ends)])  3.88 us
    ppermute x3, starting transfers between devices, fold(): lax.ppermute(low, axis, [((i + 1) % count, i) for i in range(ends)])  3.88 us
  transfers between devices with their start and end apart: 12, of which 9 were waited for; matrix products, arithmetic and copies ran while one was open for 1% of the time, Pallas kernels for 0%

profile of v1, /device:TPU:0, one launch (start us, length us, event | category | flops | bytes accessed | tf_op | source)
XLA Modules:
  0.0 135.1 jit_solution(3791595171931485327)
XLA Ops:
  0.6 0.0 copy-start
  0.6 0.0 copy-start.1
  0.7 0.0 copy-start.2
  0.7 0.8 pad_maximum_fusion.9
  1.5 4.9 %collective-permute-start = (f32[5,1,4,2,128]{4,3,2,1,0:T(2,128)S(1)}, f32[5,1,4,2,128]{4,3,2,1,0:T(2,128)S(1)}, u32[]{:S(2)}, u32[]{:S(2)}) collective-permute-start(f32[5,1,4,2,128]{4,3,2,1,0:T(2,128)S(1)} %get-tuple-element.17), channel_id=1, source_target_pairs={{0,8},{8,16},{16,24},{1,9},{9,17},{17,25},{2,10},{10,18},{18,26},{... | collective-permute-start | bytes 61448 | tf_op jit(solution)/shard_map/ppermute | solution.py:23
  6.4 1.3 collective-permute-start.1
  7.7 0.2 collective-permute-done
  7.8 4.2 %collective-permute-done.1 = f32[5,1,4,2,128]{4,3,2,1,0:T(2,128)S(1)} collective-permute-done((f32[5,1,4,2,128]{4,3,2,1,0:T(2,128)S(1)}, f32[5,1,4,2,128]{4,3,2,1,0:T(2,128)S(1)}, u32[]{:S(2)}, u32[]{:S(2)}) %collective-permute-start.1) | collective-permute-done | bytes 20512 | tf_op jit(solution)/shard_map/ppermute | solution.py:25
  12.1 0.0 copy-done
  12.1 0.0 copy-done.1
  12.1 0.0 copy-done.2
  12.1 1.3 collective-permute-start.2
  13.4 1.3 collective-permute-start.3
  14.7 0.0 collective-permute-done.2
  14.7 1.8 %collective-permute-done.3 = f32[5,6,1,2,128]{4,3,2,1,0:T(2,128)S(1)} collective-permute-done((f32[5,6,1,2,128]{4,3,2,1,0:T(2,128)S(1)}, f32[5,6,1,2,128]{4,3,2,1,0:T(2,128)S(1)}, u32[]{:S(2)}, u32[]{:S(2)}) %collective-permute-start.3) | collective-permute-done | bytes 30752 | tf_op jit(solution)/shard_map/ppermute | solution.py:25
  16.5 0.1 pad_maximum_fusion.1
  16.6 0.1 fusion.6
  16.7 0.0 copy-start.4
  16.8 3.5 %collective-permute-start.4 = (f32[5,6,6,1,128]{4,3,2,1,0:T(1,128)S(1)}, f32[5,6,6,1,128]{4,3,2,1,0:T(1,128)S(1)}, u32[]{:S(2)}, u32[]{:S(2)}) collective-permute-start(f32[5,6,6,1,128]{4,3,2,1,0:T(1,128)S(1)} %get-tuple-element.9), channel_id=1, source_target_pairs={{0,1},{1,2},{2,3},{4,5},{5,6},{6,7},{8,9},{9,10},{10,11},{12,13},{... | collective-permute-start | bytes 276488 | tf_op jit(solution)/shard_map/ppermute | solution.py:23
  20.2 1.3 collective-permute-start.5
  21.5 0.0 copy-done.4
  21.6 0.0 copy-start.3
  21.6 0.6 copy-done.3
  22.2 0.3 collective-permute-done.4
  22.5 4.2 %collective-permute-done.5 = f32[5,6,6,1,128]{4,3,2,1,0:T(1,128)S(1)} collective-permute-done((f32[5,6,6,1,128]{4,3,2,1,0:T(1,128)S(1)}, f32[5,6,6,1,128]{4,3,2,1,0:T(1,128)S(1)}, u32[]{:S(2)}, u32[]{:S(2)}) %collective-permute-start.5) | collective-permute-done | bytes 92192 | tf_op jit(solution)/shard_map/ppermute | solution.py:25
  26.7 1.0 pad_maximum_fusion.border_ref
  27.7 0.9 broadcast_in_dim.14.flags_ref
  28.6 50.8 %slots.1 = (f32[144,8,128]{2,1,0:T(8,128)}, f32[864,128]{1,0:T(8,128)}) custom-call(s32[864]{0:T(1024)} %copy-done.3, f32[5,6,6,4,128]{4,3,2,1,0:T(4,128)} %pad_maximum_fusion.border_ref, f32[864,128]{1,0:T(8,128)} %broadcast_in_dim.14.flags_ref, s32[864,128]{1,0:T(8,128)} %bitcast.13, s32[864,128]{1,0:T(8,128)} %bitcast.14, f32[864,128]{1,0:T(8,128)} %bitcast.15), custom_call_target="tpu_custom_call" | custom-call | tf_op jit(solution)/shard_map/slots/pallas_call | solution.py:226
  79.5 1.0 fusion.5
  80.5 0.1 copy.14
  80.6 0.1 copy.15
  80.6 1.3 collective-permute-start.7
  81.9 27.8 %collective-permute-start.6 = (f32[6,6,1,4,128]{4,2,1,0,3:T(1,128)S(1)}, f32[6,6,1,4,128]{4,2,1,0,3:T(1,128)S(1)}, u32[]{:S(2)}, u32[]{:S(2)}) collective-permute-start(f32[6,6,1,4,128]{4,2,1,0,3:T(1,128)S(1)} %copy.14), channel_id=1, source_target_pairs={{0,1},{1,2},{2,3},{4,5},{5,6},{6,7},{8,9},{9,10},{10,11},{12,13},{... | collective-permute-start | bytes 221192 | tf_op jit(solution)/shard_map/ppermute | solution.py:40
  109.8 1.0 slice.74
  110.8 0.0 collective-permute-done.7
  110.8 1.0 collective-permute-done.6
  111.7 0.2 fusion
  111.9 1.3 collective-permute-start.8
  113.2 1.3 collective-permute-start.9
  114.5 0.0 collective-permute-done.8
  114.5 1.8 %collective-permute-done.9 = f32[6,1,2,4,128]{4,2,1,0,3:T(2,128)S(1)} collective-permute-done((f32[6,1,2,4,128]{4,2,1,0,3:T(2,128)S(1)}, f32[6,1,2,4,128]{4,2,1,0,3:T(2,128)S(1)}, u32[]{:S(2)}, u32[]{:S(2)}) %collective-permute-start.9) | collective-permute-done | bytes 24608 | tf_op jit(solution)/shard_map/ppermute | solution.py:41
  116.4 8.5 %collective-permute-start.10 = (f32[1,4,2,4,128]{4,2,1,0,3:T(2,128)S(1)}, f32[1,4,2,4,128]{4,2,1,0,3:T(2,128)S(1)}, u32[]{:S(2)}, u32[]{:S(2)}) collective-permute-start(f32[1,4,2,4,128]{4,2,1,0,3:T(2,128)S(1)} %get-tuple-element.15), channel_id=1, source_target_pairs={{0,8},{8,16},{16,24},{1,9},{9,17},{17,25},{2,10},{10,18},{18,26},{... | collective-permute-start | bytes 49160 | tf_op jit(solution)/shard_map/ppermute | solution.py:40
  124.9 1.3 collective-permute-start.11
  126.2 0.1 collective-permute-done.10
  126.3 7.5 %collective-permute-done.11 = f32[1,4,2,4,128]{4,2,1,0,3:T(2,128)S(1)} collective-permute-done((f32[1,4,2,4,128]{4,2,1,0,3:T(2,128)S(1)}, f32[1,4,2,4,128]{4,2,1,0,3:T(2,128)S(1)}, u32[]{:S(2)}, u32[]{:S(2)}) %collective-permute-start.11) | collective-permute-done | bytes 16416 | tf_op jit(solution)/shard_map/ppermute | solution.py:41
  133.8 0.6 fusion.4
  134.4 0.6 slice.83
  (7 shorter events, 0.1 us)
Async XLA Ops:
  0.6 11.4 %copy-start = (f32[3,4,4,2,128]{4,3,2,1,0:T(2,128)S(1)}, f32[3,4,4,2,128]{4,3,2,1,0:T(2,128)}, u32[]{:S(2)}) copy-start(f32[3,4,4,2,128]{4,3,2,1,0:T(2,128)} %param.7) | copy-start | bytes 147460
  0.6 11.4 %copy-start.1 = (f32[4,4,2,128]{3,2,1,0:T(2,128)S(1)}, f32[4,4,2,128]{3,2,1,0:T(2,128)}, u32[]{:S(2)}) copy-start(f32[4,4,2,128]{3,2,1,0:T(2,128)} %param.9) | copy-start | bytes 49156
  0.7 11.4 %copy-start.2 = (f32[4,4,2,128]{3,2,1,0:T(2,128)S(1)}, f32[4,4,2,128]{3,2,1,0:T(2,128)}, u32[]{:S(2)}) copy-start(f32[4,4,2,128]{3,2,1,0:T(2,128)} %param.8) | copy-start | bytes 49156
  1.5 6.3 %collective-permute-start = (f32[5,1,4,2,128]{4,3,2,1,0:T(2,128)S(1)}, f32[5,1,4,2,128]{4,3,2,1,0:T(2,128)S(1)}, u32[]{:S(2)}, u32[]{:S(2)}) collective-permute-start(f32[5,1,4,2,128]{4,3,2,1,0:T(2,128)S(1)} %get-tuple-element.17), channel_id=1, source_target_pairs={{0,8},{8,16},{16,24},{1,9},{9,17},{17,25},{2,10},{10,18},{18,26},{... | collective-permute-start | bytes 61448 | tf_op jit(solution)/shard_map/ppermute | solution.py:23
  6.4 5.7 %collective-permute-start.1 = (f32[5,1,4,2,128]{4,3,2,1,0:T(2,128)S(1)}, f32[5,1,4,2,128]{4,3,2,1,0:T(2,128)S(1)}, u32[]{:S(2)}, u32[]{:S(2)}) collective-permute-start(f32[5,1,4,2,128]{4,3,2,1,0:T(2,128)S(1)} %get-tuple-element.18), channel_id=1, source_target_pairs={{8,0},{16,8},{24,16},{9,1},{17,9},{25,17},{10,2},{18,10},{26,18},{... | collective-permute-start | bytes 61448 | tf_op jit(solution)/shard_map/ppermute | solution.py:25
  12.1 2.6 %collective-permute-start.2 = (f32[5,6,1,2,128]{4,3,2,1,0:T(2,128)S(1)}, f32[5,6,1,2,128]{4,3,2,1,0:T(2,128)S(1)}, u32[]{:S(2)}, u32[]{:S(2)}) collective-permute-start(f32[5,6,1,2,128]{4,3,2,1,0:T(2,128)S(1)} %get-tuple-element.13), channel_id=1, source_target_pairs={{0,4},{1,5},{2,6},{3,7},{8,12},{9,13},{10,14},{11,15},{16,20},{17,... | collective-permute-start | bytes 92168 | tf_op jit(solution)/shard_map/ppermute | solution.py:23
  13.4 3.1 %collective-permute-start.3 = (f32[5,6,1,2,128]{4,3,2,1,0:T(2,128)S(1)}, f32[5,6,1,2,128]{4,3,2,1,0:T(2,128)S(1)}, u32[]{:S(2)}, u32[]{:S(2)}) collective-permute-start(f32[5,6,1,2,128]{4,3,2,1,0:T(2,128)S(1)} %get-tuple-element.14), channel_id=1, source_target_pairs={{4,0},{5,1},{6,2},{7,3},{12,8},{13,9},{14,10},{15,11},{20,16},{21,... | collective-permute-start | bytes 92168 | tf_op jit(solution)/shard_map/ppermute | solution.py:25
  16.7 4.8 %copy-start.4 = (s32[1,1,1,864]{3,2,1,0:T(1,128)S(1)}, s32[1,1,1,864]{3,2,1,0:T(1,128)}, u32[]{:S(2)}) copy-start(s32[1,1,1,864]{3,2,1,0:T(1,128)} %param.10) | copy-start | bytes 10372
  16.8 5.7 %collective-permute-start.4 = (f32[5,6,6,1,128]{4,3,2,1,0:T(1,128)S(1)}, f32[5,6,6,1,128]{4,3,2,1,0:T(1,128)S(1)}, u32[]{:S(2)}, u32[]{:S(2)}) collective-permute-start(f32[5,6,6,1,128]{4,3,2,1,0:T(1,128)S(1)} %get-tuple-element.9), channel_id=1, source_target_pairs={{0,1},{1,2},{2,3},{4,5},{5,6},{6,7},{8,9},{9,10},{10,11},{12,13},{... | collective-permute-start | bytes 276488 | tf_op jit(solution)/shard_map/ppermute | solution.py:23
  20.2 6.4 %collective-permute-start.5 = (f32[5,6,6,1,128]{4,3,2,1,0:T(1,128)S(1)}, f32[5,6,6,1,128]{4,3,2,1,0:T(1,128)S(1)}, u32[]{:S(2)}, u32[]{:S(2)}) collective-permute-start(f32[5,6,6,1,128]{4,3,2,1,0:T(1,128)S(1)} %get-tuple-element.10), channel_id=1, source_target_pairs={{1,0},{2,1},{3,2},{5,4},{6,5},{7,6},{9,8},{10,9},{11,10},{13,12},{... | collective-permute-start | bytes 276488 | tf_op jit(solution)/shard_map/ppermute | solution.py:25
  21.6 0.6 copy-start.3
  80.6 30.1 %collective-permute-start.7 = (f32[6,6,1,4,128]{4,2,1,0,3:T(1,128)S(1)}, f32[6,6,1,4,128]{4,2,1,0,3:T(1,128)S(1)}, u32[]{:S(2)}, u32[]{:S(2)}) collective-permute-start(f32[6,6,1,4,128]{4,2,1,0,3:T(1,128)S(1)} %copy.15), channel_id=1, source_target_pairs={{1,0},{2,1},{3,2},{5,4},{6,5},{7,6},{9,8},{10,9},{11,10},{13,12},{... | collective-permute-start | bytes 221192 | tf_op jit(solution)/shard_map/ppermute | solution.py:41
  81.9 29.8 %collective-permute-start.6 = (f32[6,6,1,4,128]{4,2,1,0,3:T(1,128)S(1)}, f32[6,6,1,4,128]{4,2,1,0,3:T(1,128)S(1)}, u32[]{:S(2)}, u32[]{:S(2)}) collective-permute-start(f32[6,6,1,4,128]{4,2,1,0,3:T(1,128)S(1)} %copy.14), channel_id=1, source_target_pairs={{0,1},{1,2},{2,3},{4,5},{5,6},{6,7},{8,9},{9,10},{10,11},{12,13},{... | collective-permute-start | bytes 221192 | tf_op jit(solution)/shard_map/ppermute | solution.py:40
  111.9 2.6 %collective-permute-start.8 = (f32[6,1,2,4,128]{4,2,1,0,3:T(2,128)S(1)}, f32[6,1,2,4,128]{4,2,1,0,3:T(2,128)S(1)}, u32[]{:S(2)}, u32[]{:S(2)}) collective-permute-start(f32[6,1,2,4,128]{4,2,1,0,3:T(2,128)S(1)} %get-tuple-element.11), channel_id=1, source_target_pairs={{0,4},{1,5},{2,6},{3,7},{8,12},{9,13},{10,14},{11,15},{16,20},{17,... | collective-permute-start | bytes 73736 | tf_op jit(solution)/shard_map/ppermute | solution.py:40
  113.2 3.1 %collective-permute-start.9 = (f32[6,1,2,4,128]{4,2,1,0,3:T(2,128)S(1)}, f32[6,1,2,4,128]{4,2,1,0,3:T(2,128)S(1)}, u32[]{:S(2)}, u32[]{:S(2)}) collective-permute-start(f32[6,1,2,4,128]{4,2,1,0,3:T(2,128)S(1)} %get-tuple-element.12), channel_id=1, source_target_pairs={{4,0},{5,1},{6,2},{7,3},{12,8},{13,9},{14,10},{15,11},{20,16},{21,... | collective-permute-start | bytes 73736 | tf_op jit(solution)/shard_map/ppermute | solution.py:41
  116.4 9.9 %collective-permute-start.10 = (f32[1,4,2,4,128]{4,2,1,0,3:T(2,128)S(1)}, f32[1,4,2,4,128]{4,2,1,0,3:T(2,128)S(1)}, u32[]{:S(2)}, u32[]{:S(2)}) collective-permute-start(f32[1,4,2,4,128]{4,2,1,0,3:T(2,128)S(1)} %get-tuple-element.15), channel_id=1, source_target_pairs={{0,8},{8,16},{16,24},{1,9},{9,17},{17,25},{2,10},{10,18},{18,26},{... | collective-permute-start | bytes 49160 | tf_op jit(solution)/shard_map/ppermute | solution.py:40
  124.9 8.9 %collective-permute-start.11 = (f32[1,4,2,4,128]{4,2,1,0,3:T(2,128)S(1)}, f32[1,4,2,4,128]{4,2,1,0,3:T(2,128)S(1)}, u32[]{:S(2)}, u32[]{:S(2)}) collective-permute-start(f32[1,4,2,4,128]{4,2,1,0,3:T(2,128)S(1)} %get-tuple-element.16), channel_id=1, source_target_pairs={{8,0},{16,8},{24,16},{9,1},{17,9},{25,17},{10,2},{18,10},{26,18},{... | collective-permute-start | bytes 49160 | tf_op jit(solution)/shard_map/ppermute | solution.py:41

commit v2 on v1

--- a/solution.py
+++ b/solution.py
@@ -12,40 +12,164 @@
 FLOOR = 1e-12
 
 
-def padded(cells, sides, width):
-    for axis, dim in sides:
-        count = lax.axis_size(axis)
-        ends = count - 1
-        head = lax.slice_in_dim(cells, 0, width, axis=dim)
-        tail = lax.slice_in_dim(cells, cells.shape[dim] - width, cells.shape[dim], axis=dim)
-        cells = jnp.concatenate(
-            [
-                lax.ppermute(tail, axis, [(i, (i + 1) % count) for i in range(ends)]),
-                cells,
-                lax.ppermute(head, axis, [((i + 1) % count, i) for i in range(ends)]),
-            ],
-            axis=dim,
+def neighbours():
+    return [
+        (ex, ey, ez)
+        for ex in (-1, 0, 1)
+        for ey in (-1, 0, 1)
+        for ez in (-1, 0, 1)
+        if (ex, ey, ez) != (0, 0, 0)
+    ]
+
+
+AXES = ("gx", "gy", "gz")
+
+
+def present(offset):
+    found = None
+    for axis, shift in zip(AXES, offset):
+        if shift == 0:
+            continue
+        place = lax.axis_index(axis) + shift
+        here = (place >= 0) & (place < lax.axis_size(axis))
+        found = here if found is None else found & here
+    return found
+
+
+def device_at(offset):
+    return tuple(lax.axis_index(axis) + shift for axis, shift in zip(AXES, offset))
+
+
+def opposite(offset):
+    return tuple(-shift for shift in offset)
+
+
+def greet(offsets):
+    barrier = pltpu.get_barrier_semaphore()
+    count = jnp.int32(0)
+    for offset in offsets:
+        here = present(offset)
+        count = count + here.astype(jnp.int32)
+
+        @pl.when(here)
+        def _():
+            pl.semaphore_signal(
+                barrier, inc=1, device_id=device_at(offset), device_id_type=pl.DeviceIdType.MESH
+            )
+
+    pl.semaphore_wait(barrier, count)
+
+
+def cut(offset, extents, low, whole, high):
+    pick = []
+    for shift, extent in zip(offset, extents):
+        if shift < 0:
+            pick.append(pl.ds(low(extent), 1))
+        elif shift > 0:
+            pick.append(pl.ds(high(extent), 1))
+        else:
+            pick.append(pl.ds(whole, extent))
+    return tuple(pick)
+
+
+def rim(offset, extents):
+    return cut(offset, extents, lambda n: 0, 1, lambda n: n + 1)
+
+
+def edge(offset, extents):
+    return cut(offset, extents, lambda n: 0, 0, lambda n: n - 1)
+
+
+def spread_kernel(extents, state_ref, border_ref, send_sem, recv_sem):
+    offsets = neighbours()
+    greet(offsets)
+    copies = []
+    for i, offset in enumerate(offsets):
+        copy = pltpu.make_async_remote_copy(
+            src_ref=state_ref.at[edge(offset, extents)],
+            dst_ref=border_ref.at[rim(opposite(offset), extents)],
+            send_sem=send_sem.at[i],
+            recv_sem=recv_sem.at[i],
+            device_id=device_at(offset),
+            device_id_type=pl.DeviceIdType.MESH,
         )
-    return cells
-
-
-def fold(totals, sides):
-    for axis, dim in sides:
-        count = lax.axis_size(axis)
-        ends = count - 1
-        size = totals.shape[dim]
-        low = lax.slice_in_dim(totals, 0, 1, axis=dim)
-        high = lax.slice_in_dim(totals, size - 1, size, axis=dim)
-        inner = lax.slice_in_dim(totals, 1, size - 1, axis=dim)
-        from_left = lax.ppermute(high, axis, [(i, (i + 1) % count) for i in range(ends)])
-        from_right = lax.ppermute(low, axis, [((i + 1) % count, i) for i in range(ends)])
-        length = size - 2
-        widths = [(0, 0)] * totals.ndim
-        widths[dim] = (0, length - 1)
-        other = [(0, 0)] * totals.ndim
-        other[dim] = (length - 1, 0)
-        totals = inner + jnp.pad(from_left, widths) + jnp.pad(from_right, other)
-    return totals
+        copies.append(copy)
+        pl.when(present(offset))(copy.start)
+    border_ref[rim((0, 0, 0), extents)] = state_ref[...]
+    for offset in offsets:
+
+        @pl.when(jnp.logical_not(present(offset)))
+        def _():
+            region = rim(offset, extents)
+            shape = tuple(p.size for p in region) + border_ref.shape[3:]
+            border_ref[region] = jnp.zeros(shape, jnp.float32)
+
+    for offset, copy in zip(offsets, copies):
+        pl.when(present(offset))(copy.wait_send)
+        pl.when(present(opposite(offset)))(copy.wait_recv)
+
+
+def return_kernel(extents, totals_ref, out_ref, *scratch):
+    offsets = neighbours()
+    inbox, (send_sem, recv_sem) = scratch[:-2], scratch[-2:]
+    greet(offsets)
+    copies = []
+    for i, offset in enumerate(offsets):
+        copy = pltpu.make_async_remote_copy(
+            src_ref=totals_ref.at[rim(offset, extents)],
+            dst_ref=inbox[i],
+            send_sem=send_sem.at[i],
+            recv_sem=recv_sem.at[i],
+            device_id=device_at(offset),
+            device_id_type=pl.DeviceIdType.MESH,
+        )
+        copies.append(copy)
+        pl.when(present(offset))(copy.start)
+    out_ref[...] = totals_ref[rim((0, 0, 0), extents)]
+    for i, (offset, copy) in enumerate(zip(offsets, copies)):
+
+        @pl.when(present(opposite(offset)))
+        def _():
+            copy.wait_recv()
+            region = edge(opposite(offset), extents)
+            out_ref[region] = out_ref[region] + inbox[i][...]
+
+    for offset, copy in zip(offsets, copies):
+        pl.when(present(offset))(copy.wait_send)
+
+
+def spread(state, extents):
+    sems = pltpu.SemaphoreType.DMA((26,))
+    vmem = pl.BlockSpec(memory_space=pltpu.VMEM)
+    shape = tuple(n + 2 for n in extents) + state.shape[3:]
+    return pl.pallas_call(
+        functools.partial(spread_kernel, extents),
+        out_shape=jax.ShapeDtypeStruct(shape, jnp.float32),
+        in_specs=[vmem],
+        out_specs=vmem,
+        scratch_shapes=[sems, sems],
+        compiler_params=pltpu.CompilerParams(collective_id=0, has_side_effects=True),
+        name="spread",
+    )(state)
+
+
+def collect(totals, extents):
+    sems = pltpu.SemaphoreType.DMA((26,))
+    vmem = pl.BlockSpec(memory_space=pltpu.VMEM)
+    tail = totals.shape[3:]
+    boxes = [
+        pltpu.VMEM(tuple(1 if e else n for e, n in zip(offset, extents)) + tail, jnp.float32)
+        for offset in neighbours()
+    ]
+    return pl.pallas_call(
+        functools.partial(return_kernel, extents),
+        out_shape=jax.ShapeDtypeStruct(tuple(extents) + tail, jnp.float32),
+        in_specs=[vmem],
+        out_specs=vmem,
+        scratch_shapes=boxes + [sems, sems],
+        compiler_params=pltpu.CompilerParams(collective_id=1, has_side_effects=True),
+        name="collect",
+    )(totals)
 
 
 def split(values):
@@ -86,12 +210,13 @@
         near[...] = jnp.zeros_like(near)
         held[...] = jnp.zeros_like(held)
         others[...] = jnp.full_like(others, 1.0)
-        for ix in range(bx + 2):
-            for iy in range(wy):
-                base = (ix * wy + iy) * wz
-                for c in range(5):
-                    rows[c, base : base + wz, :] = border_ref[c, ix, iy]
-                rows[5, base : base + wz, :] = 1.0 / jnp.maximum(border_ref[3, ix, iy], 0.1)
+
+        def arrange(cell, carry):
+            for c in range(6):
+                rows[c, pl.ds(cell, 1), :] = border_ref[cell, c : c + 1, :]
+            return carry
+
+        lax.fori_loop(0, cells, arrange, 0)
 
     def tile_step(local, carry):
         iy = local // bz
@@ -204,7 +329,7 @@
             for c in range(3):
                 total = jnp.sum(far[cell, c], axis=0, keepdims=True)
                 value = value - jnp.where(row == c, total, 0.0)
-            totals_ref[cell] = value
+            totals_ref[cell] = value[0:4]
             return carry
 
         lax.fori_loop(0, cells, finish, 0)
@@ -215,9 +340,12 @@
     tiles = bx * by * bz
     slots = 27 * tiles
     cells = (bx + 2) * (by + 2) * (bz + 2)
-    state = jnp.concatenate([positions, grain_radii[None], film_liquid[None]], axis=0)
-    sides = (("gx", 1), ("gy", 2), ("gz", 3))
-    border = padded(state, sides, 1)
+    extents = (bx, by, bz)
+    zero = jnp.zeros_like(grain_radii)
+    parts = [positions[c] for c in range(3)]
+    parts += [grain_radii, film_liquid, 1.0 / grain_radii, zero, zero]
+    state = jnp.stack(parts, axis=3)
+    border = spread(state, extents).reshape(cells, 8, grains)
     live = pair_live.reshape(slots)
     flags = jnp.broadcast_to(live.astype(jnp.float32)[:, None], (slots, grains))
     span = 27 * by * bz
@@ -229,13 +357,13 @@
             num_scalar_prefetch=1,
             grid=(bx,),
             in_specs=[
-                pl.BlockSpec(border.shape, lambda i, _: (0, 0, 0, 0, 0)),
+                pl.BlockSpec(border.shape, lambda i, _: (0, 0, 0)),
                 wide,
                 wide,
                 wide,
                 wide,
             ],
-            out_specs=[pl.BlockSpec((cells, 8, grains), lambda i, _: (0, 0, 0)), wide],
+            out_specs=[pl.BlockSpec((cells, 4, grains), lambda i, _: (0, 0, 0)), wide],
             scratch_shapes=[
                 pltpu.VMEM((6, height, grains), jnp.float32),
                 pltpu.VMEM((5, grains, grains), jnp.float32),
@@ -248,7 +376,7 @@
             ],
         ),
         out_shape=[
-            jax.ShapeDtypeStruct((cells, 8, grains), jnp.float32),
+            jax.ShapeDtypeStruct((cells, 4, grains), jnp.float32),
             jax.ShapeDtypeStruct((slots, grains), jnp.float32),
         ],
         name="slots",
@@ -260,8 +388,8 @@
         rupture.reshape(slots, grains),
         volume.reshape(slots, grains),
     )
-    totals = totals.reshape(bx + 2, by + 2, bz + 2, 8, grains)[:, :, :, :4]
-    folded = fold(totals, (("gz", 2), ("gy", 1), ("gx", 0))).transpose(3, 0, 1, 2, 4)
+    totals = totals.reshape(bx + 2, by + 2, bz + 2, 4, grains)
+    folded = collect(totals, extents).transpose(3, 0, 1, 2, 4)
     return (folded[:3], film_liquid + folded[3], fresh.reshape(1, 1, 1, slots, grains))
 
 

time: 137 us -> 105 us (0.77); the launches traced: 135 us -> 106 us
  starting transfers between devices: 55 us -> 0 us
  Pallas kernels: 50.8 us -> 98.6 us
  waiting for transfers between devices: 21 us -> 0 us
  other arithmetic: 2.8 us -> 1.34 us
    pallas_call x0 -> x2, Pallas kernels: none -> 59.1 us  [the longest x1 48.5 us: collect(): pl.pallas_call(functools.partial(return_kernel, extents), out_shape=jax.S...]
    ppermute x12 -> x0, starting transfers between devices: 55 us -> none  [the longest x3 37.6 us: fold(): lax.ppermute(high, axis, [(i, (i + 1) % count) for i in range(ends)])]
    ppermute x12 -> x0, waiting for transfers between devices: 21 us -> none  [the longest x3 10.2 us: padded(): lax.ppermute(head, axis, [((i + 1) % count, i) for i in range(ends)])]
    pallas_call x1, Pallas kernels: 50.8 us -> 39.5 us  [shards(): pl.pallas_call(functools.partial(kernel, (bx, by, bz, grains)), grid_spec...]
    slice x6 -> x2, local copies, waits for them, and re-layouts: 2.79 us -> 1.68 us  [the longest x1 0.92 us: shards(): folded[3]]
  transfers between devices with their start and end apart: 12 -> 0, of which waited for: 9 -> 0; matrix products, arithmetic and copies ran while one was open for 1% -> 0% of each run, Pallas kernels for 0% -> 0%
where the time goes in v2:
time: 105 us; the launch traced here: 106 us
  Pallas kernels  98.6 us (94%)
  local copies, waits for them, and re-layouts  5.35 us (5%)
  other arithmetic  1.34 us (1%)
    pallas_call x1, Pallas kernels, collect(): pl.pallas_call(functools.partial(return_kernel, extents), out_shape=jax.S...  48.5 us
    pallas_call x1, Pallas kernels, shards(): pl.pallas_call(functools.partial(kernel, (bx, by, bz, grains)), grid_spec...  39.5 us
    pallas_call x1, Pallas kernels, spread(): pl.pallas_call(functools.partial(spread_kernel, extents), out_shape=jax.S...  10.6 us

profile of v2, /device:TPU:0, one launch (start us, length us, event | category | flops | bytes accessed | tf_op | source)
XLA Modules:
  0.0 106.0 jit_solution(18270529429470535396)
XLA Ops:
  0.6 0.0 copy-start.2
  0.6 0.7 reduce.live_smem
  1.3 0.0 copy-start.3
  1.4 0.0 copy-done.2
  1.4 0.5 copy-done.3
  1.9 0.8 fusion
  2.7 0.0 copy-start.1
  2.7 0.7 copy-done.1
  3.4 0.8 stack.19.state_ref
  4.2 0.9 broadcast_in_dim.2.flags_ref
  5.2 10.6 %spread.1 = f32[6,6,4,8,128]{4,3,2,1,0:T(8,128)} custom-call(f32[4,4,2,8,128]{4,3,2,1,0:T(8,128)} %stack.19.state_ref), custom_call_target="tpu_custom_call" | custom-call | tf_op jit(solution)/shard_map/spread/pallas_call | solution.py:145
  15.8 39.5 %slots.1 = (f32[144,4,128]{2,1,0:T(4,128)}, f32[864,128]{1,0:T(8,128)}) custom-call(s32[864]{0:T(1024)} %copy-done.3, f32[144,8,128]{2,1,0:T(8,128)} %bitcast.15, f32[864,128]{1,0:T(8,128)} %broadcast_in_dim.2.flags_ref, s32[864,128]{1,0:T(8,128)} %bitcast.16, s32[864,128]{1,0:T(8,128)} %bitcast.17, f32[864,128]{1,0:T(8,128)} %bitcast.18), custom_call_target="tpu_custom_call" | custom-call | tf_op jit(solution)/shard_map/slots/pallas_call | solution.py:354
  55.3 48.5 %collect.1 = f32[4,4,2,4,128]{4,3,2,1,0:T(4,128)} custom-call(f32[6,6,4,4,128]{4,3,2,1,0:T(4,128)} %bitcast.21), custom_call_target="tpu_custom_call" | custom-call | tf_op jit(solution)/shard_map/collect/pallas_call | solution.py:164
  103.8 0.0 copy-start
  103.8 0.9 slice.21
  104.7 0.6 add.3
  105.4 0.0 copy-done
  105.4 0.6 copy.10
  (3 shorter events, 0.0 us)
Async XLA Ops:
  0.6 0.7 copy-start.2
  1.3 0.6 copy-start.3
  2.7 0.7 copy-start.1
  103.8 1.6 %copy-start = (f32[4,4,2,4,128]{4,3,2,1,0:T(4,128)S(1)}, f32[4,4,2,4,128]{4,3,2,1,0:T(4,128)}, u32[]{:S(2)}) copy-start(f32[4,4,2,4,128]{4,3,2,1,0:T(4,128)} %collect.1) | copy-start | bytes 196612

commit v3 on v2

--- a/solution.py
+++ b/solution.py
@@ -9,6 +9,9 @@
 
 ABSORB = 0.02
 TINY = 1e-30
+RADIUS_MAX = 0.6
+SLACK = 4e-3
+AWAY = -1e4
 FLOOR = 1e-12
 
 
@@ -196,6 +199,7 @@
     far,
     near,
     listed,
+    meets,
 ):
     bx, by, bz, grains = dims
     wy, wz = by + 2, bz + 2
@@ -217,16 +221,29 @@
             return carry
 
         lax.fori_loop(0, cells, arrange, 0)
+        for c in range(6):
+            idle = AWAY if c < 3 else 0.5
+            rows[c, cells : cells + 1, :] = jnp.full((1, grains), idle, jnp.float32)
+
+    slot_of = lax.broadcasted_iota(jnp.int32, (27, grains), 0)
+    up = (slot_of >= 9).astype(jnp.int32) + (slot_of >= 18).astype(jnp.int32)
+    rest = slot_of - 9 * up
+    over = (rest >= 3).astype(jnp.int32) + (rest >= 6).astype(jnp.int32)
+    shifts = [(n - 1).astype(jnp.float32) for n in (up, over, rest - 3 * over)]
+    length = jnp.sqrt(jnp.maximum(sum(e * e for e in shifts), 1.0))
+    reach = 2.0 * RADIUS_MAX * length + SLACK
+    weights = []
+    for part in range(2):
+        place = slot_of - 14 * part
+        inside = (place >= 0) & (place < 14)
+        power = jnp.left_shift(1, jnp.where(inside, place, 0)).astype(jnp.float32)
+        weights.append(jnp.where(inside, power, 0.0))
 
     def tile_step(local, carry):
         iy = local // bz
         iz = local % bz
         cell = ((step + 1) * wy + iy + 1) * wz + iz + 1
         first = local * 27
-        count = jnp.int32(0)
-        for s in range(27):
-            listed[count] = s
-            count = count + live_smem[(step * plane + local) * 27 + s]
         own = [rows[c, pl.ds(cell, 1), :] for c in range(6)]
         pad_rows = jnp.zeros((2, grains), jnp.float32)
         columns = jnp.concatenate([own[0], own[1], own[2], own[3], own[5], own[4], pad_rows], 0).T
@@ -239,6 +256,22 @@
                 for c in range(5):
                     others[c, at : at + 3, :] = rows[c, pl.ds(start, 3), :]
         partner = partner_ref[pl.ds(first, 27), :]
+        ahead = sum(e * others[c, 0:27, :] for c, e in enumerate(shifts))
+        behind = sum(e * own[c] for c, e in enumerate(shifts))
+        apart = jnp.min(ahead, axis=1, keepdims=True) - jnp.max(behind, axis=1, keepdims=True)
+        touching = apart < reach[:, 0:1]
+        bits = [
+            jnp.sum(jnp.where(touching, w[:, 0:1], 0.0), axis=0, keepdims=True).astype(jnp.int32)[0, 0]
+            for w in weights
+        ]
+        count = jnp.int32(0)
+        touch_count = jnp.int32(0)
+        for s in range(27):
+            live = live_smem[(step * plane + local) * 27 + s]
+            listed[count] = s
+            count = count + live
+            meets[touch_count] = s
+            touch_count = touch_count + live * ((bits[s // 14] >> (s % 14)) & 1)
         got = [jnp.take_along_axis(others[c, 0:27, :], partner, axis=1) for c in range(5)]
         gap = [own[c] - got[c] for c in range(3)]
         spacing = jnp.sqrt(gap[0] * gap[0] + gap[1] * gap[1] + gap[2] * gap[2])
@@ -264,42 +297,68 @@
         acc[...] = jnp.zeros_like(acc)
         lanes = lax.broadcasted_iota(jnp.int32, (grains, grains), 0)
 
+        def cell_of(s):
+            place = cell + (s // 9 - 1) * (wy * wz) + (s // 3 % 3 - 1) * wz + (s % 3 - 1)
+            return jnp.where(s == 27, cells, place)
+
         def slot_step(k, carry):
-            s = listed[k]
-            target = cell + (s // 9 - 1) * (wy * wz) + (s // 3 % 3 - 1) * wz + (s % 3 - 1)
-            values = held[pl.ds(pl.multiple_of(s * 8, 8), 8), :]
-            high, low = split(values)
-            chosen = (lanes == partner_ref[pl.ds(first + s, 1), :]).astype(jnp.float32)
-            moved = lax.dot_general(
-                jnp.concatenate([high, low], 0),
-                chosen.astype(jnp.bfloat16),
-                (((1,), (1,)), ((), ())),
-                preferred_element_type=jnp.float32,
-            )
-            near[target] += moved[0:8] + moved[8:16]
-            x, y, z, r, q = [
-                jnp.broadcast_to(rows[c, pl.ds(target, 1), :], (8, grains)) for c in (0, 1, 2, 3, 5)
-            ]
-            sums = [jnp.zeros((8, grains), jnp.float32)] * 3
+            moves = []
+            for n in range(3):
+                at = 3 * k + n
+                s = jnp.where(at < count, listed[at], 27)
+                values = held[pl.ds(pl.multiple_of(s * 8, 8), 8), :]
+                high, low = split(values)
+                line = jnp.minimum(first + s, 27 * plane - 1)
+                chosen = (lanes == partner_ref[pl.ds(line, 1), :]).astype(jnp.float32)
+                moved = lax.dot_general(
+                    jnp.concatenate([high, low], 0),
+                    chosen.astype(jnp.bfloat16),
+                    (((1,), (1,)), ((), ())),
+                    preferred_element_type=jnp.float32,
+                )
+                moves.append((cell_of(s), moved))
+            targets, keeps, fields, sums = [], [], [], []
+            for n in range(2):
+                at = 2 * k + n
+                s = jnp.where(at < touch_count, meets[at], 27)
+                target = cell_of(s)
+                targets.append(target)
+                keeps.append(jnp.where(s == 13, 0.0, 1.0))
+                fields.append(
+                    [
+                        jnp.broadcast_to(rows[c, pl.ds(target, 1), :], (8, grains))
+                        for c in (0, 1, 2, 3, 5)
+                    ]
+                )
+                sums.append([jnp.zeros((8, grains), jnp.float32)] * 3)
             for m in range(blocks):
                 part = slice(8 * m, 8 * m + 8)
-                dx = table[0, part] - x
-                dy = table[1, part] - y
-                dz = table[2, part] - z
-                square = jnp.maximum(dx * dx + dy * dy + dz * dz, FLOOR)
-                inverse = lax.rsqrt(square)
-                inter = jnp.maximum(table[3, part] + r - square * inverse, TINY)
-                push = inter * inter * inverse * lax.rsqrt(inter * (table[4, part] + q))
-                for c, member in enumerate((dx, dy, dz)):
-                    product = push * member
-                    acc[c, part] += product
-                    sums[c] = sums[c] + product
-            keep = jnp.where(s == 13, 0.0, 1.0)
-            for c in range(3):
-                far[target, c] += sums[c] * keep
+                mine = [table[c, part] for c in range(5)]
+                both = [None] * 3
+                for n in range(2):
+                    x, y, z, r, q = fields[n]
+                    dx = mine[0] - x
+                    dy = mine[1] - y
+                    dz = mine[2] - z
+                    square = jnp.maximum(dx * dx + dy * dy + dz * dz, FLOOR)
+                    inverse = lax.rsqrt(square)
+                    inter = jnp.maximum(mine[3] + r - square * inverse, TINY)
+                    push = inter * inter * inverse * lax.rsqrt(inter * (mine[4] + q))
+                    for c, member in enumerate((dx, dy, dz)):
+                        product = push * member
+                        both[c] = product if both[c] is None else both[c] + product
+                        sums[n][c] = sums[n][c] + product
+                for c in range(3):
+                    acc[c, part] += both[c]
+            for n in range(2):
+                for c in range(3):
+                    far[targets[n], c] += sums[n][c] * keeps[n]
+            for target, moved in moves:
+                near[target] += moved[0:8] + moved[8:16]
             return carry
 
-        lax.fori_loop(0, count, slot_step, 0)
+        passes = jnp.maximum((touch_count + 1) // 2, (count + 2) // 3)
+        lax.fori_loop(0, passes, slot_step, 0)
         ones = jnp.ones((8, grains), jnp.bfloat16)
         row = lax.broadcasted_iota(jnp.int32, (8, grains), 0)
         added = jnp.zeros((8, grains), jnp.float32)
@@ -350,7 +409,7 @@
     flags = jnp.broadcast_to(live.astype(jnp.float32)[:, None], (slots, grains))
     span = 27 * by * bz
     wide = pl.BlockSpec((span, grains), lambda i, _: (i, 0))
-    height = -(-cells // 8) * 8
+    height = cells // 8 * 8 + 8
     totals, fresh = pl.pallas_call(
         functools.partial(kernel, (bx, by, bz, grains)),
         grid_spec=pltpu.PrefetchScalarGridSpec(
@@ -370,8 +429,9 @@
                 pltpu.VMEM((5, 32, grains), jnp.float32),
                 pltpu.VMEM((8 * 32, grains), jnp.float32),
                 pltpu.VMEM((3, grains, grains), jnp.float32),
-                pltpu.VMEM((cells, 3, 8, grains), jnp.float32),
-                pltpu.VMEM((cells, 8, grains), jnp.float32),
+                pltpu.VMEM((cells + 1, 3, 8, grains), jnp.float32),
+                pltpu.VMEM((cells + 1, 8, grains), jnp.float32),
+                pltpu.SMEM((48,), jnp.int32),
                 pltpu.SMEM((32,), jnp.int32),
             ],
         ),

time: 105 us -> 81 us (0.77); the launches traced: 106 us -> 80.7 us
  Pallas kernels: 98.6 us -> 73.3 us
    pallas_call x1, Pallas kernels: 48.5 us -> 26.9 us  [collect(): pl.pallas_call(functools.partial(return_kernel, extents), out_shape=jax.S...]
    pallas_call x1, Pallas kernels: 39.5 us -> 35.9 us  [shards(): pl.pallas_call(functools.partial(kernel, (bx, by, bz, grains)), grid_spec...]
where the time goes in v3:
time: 81 us; the launch traced here: 80.7 us
  Pallas kernels  73.3 us (90%)
  local copies, waits for them, and re-layouts  5.35 us (7%)
  other arithmetic  1.34 us (2%)
    pallas_call x1, Pallas kernels, shards(): pl.pallas_call(functools.partial(kernel, (bx, by, bz, grains)), grid_spec...  35.9 us
    pallas_call x1, Pallas kernels, collect(): pl.pallas_call(functools.partial(return_kernel, extents), out_shape=jax.S...  26.9 us
    pallas_call x1, Pallas kernels, spread(): pl.pallas_call(functools.partial(spread_kernel, extents), out_shape=jax.S...  10.6 us
    unnamed x9, local copies, waits for them, and re-layouts  1.9 us

profile of v3, /device:TPU:0, one launch (start us, length us, event | category | flops | bytes accessed | tf_op | source)
XLA Modules:
  0.0 80.7 jit_solution(10341789148859726157)
XLA Ops:
  0.6 0.0 copy-start.2
  0.6 0.7 reduce.live_smem
  1.3 0.0 copy-start.3
  1.4 0.0 copy-done.2
  1.4 0.5 copy-done.3
  1.9 0.8 fusion
  2.7 0.0 copy-start.1
  2.7 0.7 copy-done.1
  3.4 0.8 %stack.19.state_ref = f32[4,4,2,8,128]{4,3,2,1,0:T(8,128)} concatenate(f32[4,4,2,1,128]{4,3,2,1,0:T(1,128)S(1)} %bitcast.27, f32[4,4,2,1,128]{4,3,2,1,0:T(1,128)S(1)} %bitcast.28, f32[4,4,2,1,128]{4,3,2,1,0:T(1,128)S(1)} %bitcast.26, f32[4,4,2,1,128]{4,3,2,1,0:T(1,128)S(1)} %bitcast.23, f32[4,4,2,1,128]{4,3,2,1,0:T(1,128)S(1)} %bitcast.22, f32[4,4,2,1,128]{4,3,2,1,0:T(1,128)S(1)} %bitcast.24, ...), dimensions={3} | concatenate | bytes 262144 | tf_op jit(solution)/shard_map/stack | solution.py:406
  4.2 0.9 %broadcast_in_dim.2.flags_ref = f32[864,128]{1,0:T(8,128)} broadcast(f32[864]{0:T(1024)S(1)} %convert_element_type.7), dimensions={0} | broadcast | bytes 445824 | tf_op jit(solution)/shard_map/broadcast_in_dim | solution.py:409
  5.2 10.6 %spread.1 = f32[6,6,4,8,128]{4,3,2,1,0:T(8,128)} custom-call(f32[4,4,2,8,128]{4,3,2,1,0:T(8,128)} %stack.19.state_ref), custom_call_target="tpu_custom_call" | custom-call | tf_op jit(solution)/shard_map/spread/pallas_call | solution.py:148
  15.8 35.9 %slots.1 = (f32[144,4,128]{2,1,0:T(4,128)}, f32[864,128]{1,0:T(8,128)}) custom-call(s32[864]{0:T(1024)} %copy-done.3, f32[144,8,128]{2,1,0:T(8,128)} %bitcast.15, f32[864,128]{1,0:T(8,128)} %broadcast_in_dim.2.flags_ref, s32[864,128]{1,0:T(8,128)} %bitcast.16, s32[864,128]{1,0:T(8,128)} %bitcast.17, f32[864,128]{1,0:T(8,128)} %bitcast.18), custom_call_target="tpu_custom_call" | custom-call | tf_op jit(solution)/shard_map/slots/pallas_call | solution.py:413
  51.7 26.9 %collect.1 = f32[4,4,2,4,128]{4,3,2,1,0:T(4,128)} custom-call(f32[6,6,4,4,128]{4,3,2,1,0:T(4,128)} %bitcast.21), custom_call_target="tpu_custom_call" | custom-call | tf_op jit(solution)/shard_map/collect/pallas_call | solution.py:167
  78.5 0.0 copy-start
  78.5 0.9 %slice.21 = f32[1,4,4,2,128]{4,0,3,2,1:T(1,128)S(1)} slice(f32[4,4,4,2,128]{4,0,3,2,1:T(4,128)} %bitcast.19), slice={[3:4], [0:4], [0:4], [0:2], [0:128]} | slice | bytes 32768 | tf_op jit(solution)/shard_map/slice | solution.py:453
  79.5 0.6 add.3
  80.1 0.0 copy-done
  80.1 0.6 copy.10
  (3 shorter events, 0.0 us)
Async XLA Ops:
  0.6 0.7 copy-start.2
  1.3 0.6 copy-start.3
  2.7 0.7 copy-start.1
  78.5 1.6 %copy-start = (f32[4,4,2,4,128]{4,3,2,1,0:T(4,128)S(1)}, f32[4,4,2,4,128]{4,3,2,1,0:T(4,128)}, u32[]{:S(2)}) copy-start(f32[4,4,2,4,128]{4,3,2,1,0:T(4,128)} %collect.1) | copy-start | bytes 196612
